TPU v7x, 32 devices: a whole 2x2x4 slice. The times are simulated.
32 devices in a mesh: site: 8 (over y, x, core), scen: 4 (over z).
Axes of the slice: x: 2, y: 2, z: 4, core: 2. Of those that a mesh axis runs over, the one named last changes fastest.
Arguments:
- normals: bfloat16 [20480, 1344], P('site', 'scen'), may hold values from -6 to 6
- pattern: int32 [32, 40], replicated, may hold values from 0 to 79, as said below
- factor: bfloat16 [32, 40, 256, 256], P('site', None, 'scen'), may hold values from -0.0625 to 0.0625
- temporal: bfloat16 [168, 168], replicated, may hold values from -0.5 to 0.5
- capacity: float32 [8192], P('site'), may hold values from 0.05 to 0.4
- spread: float32 [8192], P('site'), may hold values from 0.2 to 0.8
- bus_map: int32 [8192], replicated, may hold values from 0 to 511
Outputs:
- bus_power: float32 [512, 1344], P('site', 'scen')
Inputs may be any that keep to these rules, and one draw needn't show every extreme that they name: `pattern`: each block row names 40 different column blocks. The 4 block rows of one index of site (rows k * 4 to (k + 1) * 4 - 1) name at most 5 different column blocks among those held by any one index of site (blocks j * 10 to (j + 1) * 10 - 1), and exactly 5 among those held by index k itself.
All inputs are finite; a program needn't handle non-finite values.
Results may differ from a plain program's by a relative error of at most 0.0013.
Values may be sent and summed in bfloat16 or wider, within the bound.
A program may use at most 192 MiB of HBM per device.

v0:
```python
import jax
import jax.numpy as jnp
from jax import lax
from jax.sharding import PartitionSpec as P

BLK = 256
HOURS = 168
NZ = 40
MAX_COLUMN_BLOCKS = 5
RB_DEV = 4
BUS_DEV = 64


def shards(normals, pattern, factor, temporal, capacity, spread, bus_map):
    own_index = lax.axis_index("site")
    site_count = lax.axis_size("site")
    row_width = normals.shape[1]
    scen_here = row_width // HOURS
    local_blocks = normals.reshape(-1, BLK, row_width)
    block_count = local_blocks.shape[0]
    all_blocks = block_count * site_count
    my_columns = lax.dynamic_slice_in_dim(pattern, own_index * RB_DEV, RB_DEV, 0).reshape(-1)
    block_ids = jnp.arange(all_blocks, dtype=jnp.int32)
    wanted = pattern.reshape(site_count, -1)
    needed = jnp.any(wanted[:, :, None] == block_ids[None, None, :], axis=1)
    owned_need = lax.dynamic_slice_in_dim(needed, own_index * block_count, block_count, 1).astype(
        jnp.int32
    )
    slot_rank = jnp.cumsum(owned_need, axis=1) - 1
    slot_ids = jnp.arange(MAX_COLUMN_BLOCKS, dtype=jnp.int32)
    chosen = (owned_need[:, None, :] == 1) & (slot_rank[:, None, :] == slot_ids[None, :, None])
    local_ids = jnp.arange(block_count, dtype=jnp.int32)
    block_index = jnp.sum(jnp.where(chosen, local_ids[None, None, :], 0), axis=2)
    present = jnp.any(chosen, axis=2)
    outgoing = jnp.where(
        present[:, :, None, None], local_blocks[block_index], jnp.zeros((), normals.dtype)
    )
    arrived = lax.all_to_all(outgoing, "site", split_axis=0, concat_axis=0, tiled=True)
    my_need = lax.dynamic_index_in_dim(needed, own_index, 0, keepdims=False).astype(jnp.int32)
    my_rank = (jnp.cumsum(my_need.reshape(site_count, block_count), axis=1) - 1).reshape(-1)
    slot_of = my_columns // block_count * MAX_COLUMN_BLOCKS + my_rank[my_columns]
    picked = jnp.take(
        arrived.reshape(site_count * MAX_COLUMN_BLOCKS, BLK, row_width), slot_of, axis=0
    )
    picked = picked.reshape(RB_DEV, NZ, BLK, row_width)
    capacity_rows = capacity.reshape(RB_DEV, BLK)
    spread_rows = spread.reshape(RB_DEV, BLK)
    portion = lax.all_gather(factor, "scen", axis=2, tiled=True)
    height = portion.shape[2]
    spatial = jnp.einsum(
        "ktij,ktjw->kiw", portion, picked, preferred_element_type=jnp.float32
    ).astype(jnp.bfloat16)
    hourly = spatial.reshape(RB_DEV, height, scen_here, HOURS)
    weather = jnp.einsum("kpsg,hg->kpsh", hourly, temporal, preferred_element_type=jnp.float32)
    scale_part = capacity_rows[:, :, None, None]
    spread_part = spread_rows[:, :, None, None]
    values = scale_part * jnp.exp(spread_part * weather - 0.5 * spread_part * spread_part)
    injected = (
        values.astype(jnp.bfloat16)
        .reshape(RB_DEV, height, row_width)
        .reshape(RB_DEV * BLK, row_width)
    )
    bus_ids = own_index * BUS_DEV + jnp.arange(BUS_DEV, dtype=jnp.int32)
    onehot_rows = (bus_map[None, :] == bus_ids[:, None]).astype(jnp.bfloat16)
    return jnp.dot(
        onehot_rows,
        lax.all_gather(injected, "site", axis=0, tiled=True),
        preferred_element_type=jnp.float32,
    )


def solution(mesh):
    placed = (P("site", "scen"), P(), P("site", None, "scen", None), P(), P("site"), P("site"), P())
    return jax.shard_map(
        shards, mesh=mesh, in_specs=placed, out_specs=P("site", "scen"), check_vma=False
    )
```

profile of v0, /device:TPU:0, one launch (start us, length us, event | category | flops | bytes accessed | tf_op | source)
XLA Modules:
  0.0 440.7 jit_solution(17273901269101868076)
XLA Ops:
  6.5 0.0 copy-start
  6.5 0.0 all-gather.3.cloned.1.call-start
  6.5 0.7 all-gather.3.cloned.1.call-update
  7.3 0.8 eq.51
  8.1 0.3 fusion.18
  8.3 0.1 broadcast_compare_fusion
  8.4 0.2 reduce_window_sum.18
  8.6 0.2 select_reduce_fusion
  8.7 0.1 copy.13
  8.8 0.1 reshape.181
  8.9 3.9 copy.12
  12.8 2.8 copy.14
  15.6 0.2 fusion.21
  15.8 0.1 copy.11
  15.9 6.4 %gather_fusion.1 = bf16[40,256,336]{1,2,0:T(8,128)(2,1)} fusion(bf16[10,256,336]{1,2,0:T(8,128)(2,1)S(1)} %copy.14, s32[1024]{0:T(1024)S(1)} %pad_clamp_fusion.1), kind=kCustom, calls=%fused_computation.1 | custom fusion | bytes 13762720 | tf_op jit(solution)/shard_map/gather | solution.py:36
  22.3 7.8 %broadcast_select_fusion = bf16[8,5,256,336]{2,3,1,0:T(8,128)(2,1)} fusion(bf16[8,5,256,336]{2,3,1,0:T(8,128)(2,1)} %bitcast.33, pred[8,5]{1,0:T(8,128)(4,1)S(1)} %copy.11), kind=kLoop, calls=%fused_computation.7 | loop fusion | flops 3440640 | bytes 13762600 | tf_op jit(solution)/shard_map/jit(_where)/select_n | solution.py:35
  30.1 0.0 copy-start.2
  30.1 0.0 copy-start.3
  30.1 5.1 %all-to-all-start = ((bf16[8,5,256,336]{2,3,1,0:T(8,128)(2,1)}), bf16[8,5,256,336]{2,3,1,0:T(8,128)(2,1)}, u32[]{:S(2)}, u32[]{:S(2)}) async-start(bf16[8,5,256,336]{2,3,1,0:T(8,128)(2,1)} %broadcast_select_fusion), calls=%async_computation | async-start | bytes 13762560 | tf_op jit(solution)/shard_map/all_to_all | solution.py:38
  35.2 0.0 all-gather.5.cloned.1.call-start
  35.2 0.7 constant_dynamic-slice_fusion
  35.9 0.1 reshape.166
  36.1 0.1 reshape.170
  36.1 0.2 reduce_window_sum.17
  36.3 0.1 sub.26
  36.4 1.6 gather_fusion
  38.0 0.1 gather.17
  38.1 0.0 copy-done.2
  38.1 0.0 copy-done.3
  38.1 0.7 compare_and_fusion
  38.8 74.7 %all-to-all-done = bf16[8,5,256,336]{2,3,1,0:T(8,128)(2,1)} async-done(((bf16[8,5,256,336]{2,3,1,0:T(8,128)(2,1)}), bf16[8,5,256,336]{2,3,1,0:T(8,128)(2,1)}, u32[]{:S(2)}, u32[]{:S(2)}) %all-to-all-start) | async-done | bytes 6881312 | tf_op jit(solution)/shard_map/all_to_all | solution.py:38
  113.5 15.0 %gather_fusion.2 = bf16[160,256,336]{1,2,0:T(8,128)(2,1)} fusion(bf16[40,256,336]{1,2,0:T(8,128)(2,1)} %bitcast.4, s32[1024]{0:T(1024)S(1)} %pad_clamp_fusion), kind=kCustom, calls=%fused_computation.2 | custom fusion | bytes 55050880 | tf_op jit(solution)/shard_map/jit(_take)/gather | solution.py:42
  128.5 240.0 %all-gather.3.cloned.1.call-done = bf16[4,40,256,256]{3,2,1,0:T(8,128)(2,1)} async-done(((bf16[4,40,64,256]{3,2,1,0:T(8,128)(2,1)}), bf16[4,40,256,256]{3,2,1,0:T(8,128)(2,1)}) %all-gather.3.cloned.1.call-update) | async-done | bytes 20971536 | tf_op jit(solution)/shard_map/all_gather | solution.py:48
  368.5 0.0 copy-start.1
  368.5 17.8 %fusion.13 = bf16[4,336,256]{2,1,0:T(8,128)(2,1)S(1)} fusion(bf16[4,40,256,256]{3,2,1,0:T(8,128)(2,1)} %all-gather.3.cloned.1.call-done, bf16[4,40,256,336]{2,3,1,0:T(8,128)(2,1)} %bitcast.32, pred[4,40]{1,0:T(4,128)(4,1)S(1)} %compare_and_fusion), kind=kOutput, calls=%fused_computation.16 | convolution fusion | flops 7060537344 | bytes 49184928 | tf_op jit(solution)/shard_map/ktij,ktjw->kiw/dot_general | solution.py:50
  386.3 0.0 copy-done
  386.3 0.4 fusion.12
  386.7 0.4 copy.15
  387.1 1.0 copy.18
  388.1 0.0 all-gather.5.cloned.1.call-update
  388.2 40.8 %all-gather.5.cloned.1.call-done = bf16[8192,336]{0,1:T(8,128)(2,1)} async-done(((bf16[1024,336]{0,1:T(8,128)(2,1)}), bf16[8192,336]{0,1:T(8,128)(2,1)}) %all-gather.5.cloned.1.call-update) | async-done | bytes 5505040 | tf_op jit(solution)/shard_map/all_gather | solution.py:67
  428.9 0.0 copy-done.1
  429.0 4.9 %fusion.4 = f32[64,336]{1,0:T(8,128)} fusion(bf16[8192,336]{0,1:T(8,128)(2,1)} %all-gather.5.cloned.1.call-done, s32[8192]{0:T(1024)S(1)} %copy-done.1, s32[64]{0:T(128)S(1)} %iota_add_fusion), kind=kOutput, calls=%fused_computation.8 | convolution fusion | flops 352845824 | bytes 5624064 | tf_op jit(solution)/shard_map/dot_general | solution.py:65
  (13 shorter events, 0.1 us)
Async XLA Ops:
  6.5 379.8 %copy-start = (bf16[168,168]{1,0:T(8,128)(2,1)S(1)}, bf16[168,168]{1,0:T(8,128)(2,1)}, u32[]{:S(2)}) copy-start(bf16[168,168]{1,0:T(8,128)(2,1)} %param.10) | copy-start | bytes 169348
  6.5 362.0 %all-gather.3.cloned.1.call-start = ((), (), s32[]{:S(2)}) async-start(), calls=%async_computation.1 | async-start | bytes 26214400 | tf_op jit(solution)/shard_map/all_gather | solution.py:48
  30.1 7.9 %copy-start.2 = (f32[1024]{0:T(1024)S(1)}, f32[1024]{0:T(1024)}, u32[]{:S(2)}) copy-start(f32[1024]{0:T(1024)} %param.12) | copy-start | bytes 12292
  30.1 7.9 %copy-start.3 = (f32[1024]{0:T(1024)S(1)}, f32[1024]{0:T(1024)}, u32[]{:S(2)}) copy-start(f32[1024]{0:T(1024)} %param.11) | copy-start | bytes 12292
  30.1 83.4 %all-to-all-start = ((bf16[8,5,256,336]{2,3,1,0:T(8,128)(2,1)}), bf16[8,5,256,336]{2,3,1,0:T(8,128)(2,1)}, u32[]{:S(2)}, u32[]{:S(2)}) async-start(bf16[8,5,256,336]{2,3,1,0:T(8,128)(2,1)} %broadcast_select_fusion), calls=%async_computation | async-start | bytes 13762560 | tf_op jit(solution)/shard_map/all_to_all | solution.py:38
  35.2 393.7 %all-gather.5.cloned.1.call-start = ((), (), s32[]{:S(2)}) async-start(), calls=%async_computation.2 | async-start | bytes 6193152 | tf_op jit(solution)/shard_map/all_gather | solution.py:67
  368.5 60.5 %copy-start.1 = (s32[8192]{0:T(1024)S(1)}, s32[8192]{0:T(1024)}, u32[]{:S(2)}) copy-start(s32[8192]{0:T(1024)} %param.13) | copy-start | bytes 98308
Sparse Core Ops, SparseCore 0:
  8.9 359.5 all-gather.2
  388.3 40.6 all-gather.4
where the time goes:
time: 441 us
  waiting for transfers between devices  356 us (81%)
  local copies, waits for them, and re-layouts  33.1 us (8%)
  matrix products  23.1 us (5%)
  between operations  13.5 us (3%)
  other arithmetic  9.61 us (2%)
  starting transfers between devices  5.11 us (1%)
    all_gather x1, waiting for transfers between devices, shards(): portion = lax.all_gather(factor, 'scen', axis=2, tiled=True)  240 us
    all_to_all x1, waiting for transfers between devices, shards(): lax.all_to_all(outgoing, 'site', split_axis=0, concat_axis=0, tiled=True)  74.7 us
    all_gather x1, waiting for transfers between devices, shards(): lax.all_gather(injected, 'site', axis=0, tiled=True)  40.8 us
    dot_general x1, matrix products, shards(): jnp.einsum('ktij,ktjw->kiw', portion, picked, preferred_element_type=jnp....  17.8 us
    gather x1, local copies, waits for them, and re-layouts, shards(): jnp.take(arrived.reshape(site_count * MAX_COLUMN_BLOCKS, BLK, row_width),...  15 us
  transfers between devices with their start and end apart: 3, of which 3 were waited for; matrix products, arithmetic and copies ran while one was open for 9% of the time, Pallas kernels for 0%

commit v1 on v0

v1 whole, which is shorter than its diff:
```python
import jax
import jax.numpy as jnp
from jax import lax
from jax.sharding import PartitionSpec as P

BLK = 256
HOURS = 168
NZ = 40
MAX_COLUMN_BLOCKS = 5


def shards(normals, pattern, factor, temporal, capacity, spread, bus_map, buses):
    own = lax.axis_index("site")
    sites = lax.axis_size("site")
    group = lax.axis_index("scen")
    groups = lax.axis_size("scen")
    width = normals.shape[1]
    scen_here = width // HOURS
    rows_here, _, height, _ = factor.shape
    halves = groups // 2

    partner_factor = lax.ppermute(factor, "scen", [(z, z ^ 1) for z in range(groups)])
    parts = [normals]
    for s in range(1, halves):
        parts.append(
            lax.ppermute(normals, "scen", [(z, (z + 2 * s) % groups) for z in range(groups)])
        )

    block_count = normals.shape[0] // BLK
    all_blocks = block_count * sites
    block_ids = jnp.arange(all_blocks, dtype=jnp.int32)
    wanted = pattern.reshape(sites, -1)
    needed = jnp.any(wanted[:, :, None] == block_ids[None, None, :], axis=1)
    owned_need = lax.dynamic_slice_in_dim(needed, own * block_count, block_count, 1)
    owned_need = owned_need.astype(jnp.int32)
    slot_rank = jnp.cumsum(owned_need, axis=1) - 1
    slot_ids = jnp.arange(MAX_COLUMN_BLOCKS, dtype=jnp.int32)
    chosen = (owned_need[:, None, :] == 1) & (slot_rank[:, None, :] == slot_ids[None, :, None])
    local_ids = jnp.arange(block_count, dtype=jnp.int32)
    block_index = jnp.sum(jnp.where(chosen, local_ids[None, None, :], 0), axis=2)

    my_columns = lax.dynamic_slice_in_dim(pattern, own * rows_here, rows_here, 0)
    my_need = lax.dynamic_index_in_dim(needed, own, 0, keepdims=False).astype(jnp.int32)
    my_rank = (jnp.cumsum(my_need.reshape(sites, block_count), axis=1) - 1).reshape(-1)
    slot_of_block = block_ids // block_count * MAX_COLUMN_BLOCKS + my_rank
    slots = sites * MAX_COLUMN_BLOCKS
    slot_of = jnp.sum(
        jnp.where(my_columns[:, :, None] == block_ids, slot_of_block[None, None, :], 0), axis=2
    )
    match = slot_of[:, None, :] == jnp.arange(slots, dtype=jnp.int32)[None, :, None]
    place = jnp.sum(jnp.where(match, jnp.arange(NZ, dtype=jnp.int32), 0), axis=2)
    named = jnp.any(match, axis=2)

    def in_slot_order(blocks):
        flat = blocks.reshape(rows_here * NZ, height, BLK)
        index = place + jnp.arange(rows_here, dtype=jnp.int32)[:, None] * NZ
        ordered = flat[index]
        if slots > NZ:
            ordered = jnp.where(named[:, :, None, None], ordered, jnp.zeros((), flat.dtype))
        return ordered

    ordered = [in_slot_order(factor), in_slot_order(partner_factor)]

    starts = [group * height, (group ^ 1) * height]

    def of_rows(values):
        table = values.reshape(rows_here, BLK)
        return [lax.dynamic_slice_in_dim(table, start, height, 1) for start in starts]

    scales, spreads = of_rows(capacity), of_rows(spread)
    maps = of_rows(lax.dynamic_slice_in_dim(bus_map, own * rows_here * BLK, rows_here * BLK, 0))
    bus_ids = jnp.arange(buses, dtype=jnp.int32)
    onehots = [
        (m.reshape(-1)[None, :] == bus_ids[:, None]).astype(jnp.bfloat16) for m in maps
    ]

    arrivals = []
    for part in parts:
        outgoing = part.reshape(block_count, BLK, width)[block_index]
        if arrivals:
            outgoing, arrivals[-1] = lax.optimization_barrier((outgoing, arrivals[-1]))
        arrivals.append(
            lax.all_to_all(outgoing, "site", split_axis=0, concat_axis=0, tiled=True)
        )

    totals = []
    for arrived in arrivals:
        blocks = arrived.reshape(slots, BLK, width)
        total = None
        for portion, scale, deviation, onehot in zip(ordered, scales, spreads, onehots):
            spatial = jnp.einsum(
                "ksij,sjw->kiw", portion, blocks, preferred_element_type=jnp.float32
            ).astype(jnp.bfloat16)
            hourly = spatial.reshape(rows_here, height, scen_here, HOURS)
            weather = jnp.einsum(
                "kpsg,hg->kpsh", hourly, temporal, preferred_element_type=jnp.float32
            )
            scale_part = scale[:, :, None, None]
            spread_part = deviation[:, :, None, None]
            values = scale_part * jnp.exp(spread_part * weather - 0.5 * spread_part * spread_part)
            injected = values.astype(jnp.bfloat16).reshape(rows_here * height, width)
            term = jnp.dot(onehot, injected, preferred_element_type=jnp.float32)
            total = term if total is None else total + term
        totals.append(total)

    stacked = jnp.concatenate(totals, axis=1).reshape(sites, buses // sites, -1)
    shares = lax.all_to_all(stacked, "site", split_axis=0, concat_axis=0, tiled=True)
    mine = jnp.sum(shares, axis=0)
    result = mine[:, :width]
    for s in range(1, halves):
        back = [(z, (z - 2 * s) % groups) for z in range(groups)]
        result = result + lax.ppermute(mine[:, s * width : (s + 1) * width], "scen", back)
    return result


def solution(mesh):
    placed = (P("site", "scen"), P(), P("site", None, "scen", None), P(), P("site"), P("site"), P())
    sites = mesh.shape["site"]

    def whole(normals, pattern, factor, temporal, capacity, spread, bus_map):
        buses = sites * (factor.shape[0] // sites) * BLK // 16
        body = lambda *args: shards(*args, buses)
        return jax.shard_map(
            body, mesh=mesh, in_specs=placed, out_specs=P("site", "scen"), check_vma=False
        )(normals, pattern, factor, temporal, capacity, spread, bus_map)

    return whole
```

time: 441 us -> 313 us (0.71)
  waiting for transfers between devices: 356 us -> 188 us
  blocking collectives: 0 us -> 23.4 us
  local copies, waits for them, and re-layouts: 33.1 us -> 48.9 us
  starting transfers between devices: 5.11 us -> 19 us
  between operations: 13.5 us -> 0.35 us
  other arithmetic: 9.61 us -> 2.27 us
  matrix products: 23.1 us -> 29.9 us
    all_gather x2 -> x0, waiting for transfers between devices: 281 us -> none  [the longest x1 240 us: shards(): portion = lax.all_gather(factor, 'scen', axis=2, tiled=True)]
    ppermute x0 -> x3, waiting for transfers between devices: none -> 151 us  [the longest x1 147 us: shards(): lax.ppermute(normals, 'scen', [(z, (z + 2 * s) % groups) for z in range(g...]
    all_to_all x1 -> x2, waiting for transfers between devices: 74.7 us -> 37.5 us  [shards(): lax.all_to_all(outgoing, 'site', split_axis=0, concat_axis=0, tiled=True)]
    all_to_all x0 -> x1, blocking collectives: none -> 23.4 us  [shards(): lax.all_to_all(stacked, 'site', split_axis=0, concat_axis=0, tiled=True)]
    ppermute x0 -> x3, starting transfers between devices: none -> 8.8 us  [the longest x1 3.45 us: shards(): lax.ppermute(mine[:, s * width:(s + 1) * width], 'scen', back)]
    gather x4, local copies, waits for them, and re-layouts: 23 us -> 31.3 us  [the longest x2 20.5 us: in_slot_order(): ordered = flat[index]]
    select_n x4 -> x2, other arithmetic: 7.83 us -> 0.08 us  [the longest x1 0.07 us: in_slot_order(): ordered = flat[index]]
    dot_general x2 -> x8, matrix products: 22.7 us -> 28.7 us  [the longest x4 27.4 us: shards(): jnp.einsum('ksij,sjw->kiw', portion, blocks, preferred_element_type=jnp.f...]
  transfers between devices with their start and end apart: 3 -> 5, of which waited for: 3 -> 3; matrix products, arithmetic and copies ran while one was open for 9% -> 16% of each run, Pallas kernels for 0% -> 0%
where the time goes in v1:
time: 313 us; the launch traced here: 312 us
  waiting for transfers between devices  188 us (60%)
  local copies, waits for them, and re-layouts  48.9 us (16%)
  matrix products  29.9 us (10%)
  blocking collectives  23.4 us (7%)
  starting transfers between devices  19 us (6%)
    ppermute x1, waiting for transfers between devices, shards(): lax.ppermute(normals, 'scen', [(z, (z + 2 * s) % groups) for z in range(g...  147 us
    all_to_all x2, waiting for transfers between devices, shards(): lax.all_to_all(outgoing, 'site', split_axis=0, concat_axis=0, tiled=True)  37.5 us
    dot_general x4, matrix products, shards(): jnp.einsum('ksij,sjw->kiw', portion, blocks, preferred_element_type=jnp.f...  27.4 us
    all_to_all x1, blocking collectives, shards(): lax.all_to_all(stacked, 'site', split_axis=0, concat_axis=0, tiled=True)  23.4 us
    gather x2, local copies, waits for them, and re-layouts, in_slot_order(): ordered = flat[index]  20.5 us
    gather x2, local copies, waits for them, and re-layouts, shards(): outgoing = part.reshape(block_count, BLK, width)[block_index]  10.8 us
    all_to_all x2, starting transfers between devices, shards(): lax.all_to_all(outgoing, 'site', split_axis=0, concat_axis=0, tiled=True)  10.2 us
  transfers between devices with their start and end apart: 5, of which 3 were waited for; matrix products, arithmetic and copies ran while one was open for 16% of the time, Pallas kernels for 0%

profile of v1, /device:TPU:0, one launch (start us, length us, event | category | flops | bytes accessed | tf_op | source)
XLA Modules:
  0.0 312.3 jit_solution(5202854225791556208)
XLA Ops:
  0.0 0.8 eq.98
  0.8 0.3 fusion.20
  1.1 0.1 broadcast_compare_fusion
  1.2 0.2 reduce_window_sum.18
  1.3 0.2 select_reduce_fusion.2
  1.5 0.1 copy.28
  1.6 0.1 reshape.190
  1.7 3.9 %copy.30 = bf16[2560,336]{1,0:T(8,128)(2,1)} copy(bf16[2560,336]{0,1:T(8,128)(2,1)} %param.7) | data formatting | bytes 3440640 | tf_op args[0]
  5.6 2.8 copy.31
  8.4 5.5 %gather_fusion.2 = bf16[40,256,336]{1,2,0:T(8,128)(2,1)} fusion(bf16[10,256,336]{1,2,0:T(8,128)(2,1)S(1)} %copy.31, s32[1024]{0:T(1024)S(1)} %pad_clamp_fusion), kind=kCustom, calls=%fused_computation.2 | custom fusion | bytes 13762720 | tf_op jit(solution)/shard_map/gather | solution.py:79
  13.9 5.3 %all-to-all-start = ((bf16[8,5,256,336]{2,3,1,0:T(8,128)(2,1)}), bf16[8,5,256,336]{2,3,1,0:T(8,128)(2,1)}, u32[]{:S(2)}, u32[]{:S(2)}) async-start(bf16[8,5,256,336]{2,3,1,0:T(8,128)(2,1)} %bitcast.69), calls=%async_computation | async-start | bytes 13762560 | tf_op jit(solution)/shard_map/all_to_all | solution.py:83
  19.1 2.8 collective-permute-start.1
  21.9 2.6 collective-permute-start
  24.5 147.3 %collective-permute-done = bf16[2560,336]{0,1:T(8,128)(2,1)S(1)} collective-permute-done((bf16[2560,336]{0,1:T(8,128)(2,1)S(1)}, bf16[2560,336]{0,1:T(8,128)(2,1)S(1)}, u32[]{:S(2)}, u32[]{:S(2)}) %collective-permute-start) | collective-permute-done | bytes 1720352 | tf_op jit(solution)/shard_map/ppermute | solution.py:26
  171.8 2.5 copy.27
  174.2 2.8 copy.29
  177.0 5.4 %gather_fusion.1 = bf16[40,256,336]{1,2,0:T(8,128)(2,1)} fusion(bf16[10,256,336]{1,2,0:T(8,128)(2,1)S(1)} %copy.29, s32[1024]{0:T(1024)S(1)} %pad_clamp_fusion), kind=kCustom, calls=%fused_computation.1 | custom fusion | bytes 13762720 | tf_op jit(solution)/shard_map/gather | solution.py:79
  182.4 4.9 %all-to-all-start.1 = ((bf16[8,5,256,336]{2,3,1,0:T(8,128)(2,1)}), bf16[8,5,256,336]{2,3,1,0:T(8,128)(2,1)}, u32[]{:S(2)}, u32[]{:S(2)}) async-start(bf16[8,5,256,336]{2,3,1,0:T(8,128)(2,1)} %bitcast.68), calls=%async_computation.1 | async-start | bytes 13762560 | tf_op jit(solution)/shard_map/all_to_all | solution.py:83
  187.4 0.1 reshape.179
  187.5 0.2 reduce_window_sum.17
  187.6 0.1 sub.44
  187.7 0.7 constant_dynamic-slice_fusion.4
  188.4 0.2 select_reduce_fusion.1
  188.7 0.2 select_reduce_fusion
  188.9 0.1 reshape.182
  189.0 0.7 dynamic_slice.31
  189.8 0.1 eq.91
  189.9 0.1 eq.110
  190.0 10.3 %gather_fusion = bf16[160,64,256]{2,1,0:T(8,128)(2,1)} fusion(bf16[160,64,256]{2,1,0:T(8,128)(2,1)} %bitcast.73, s32[1024]{0:T(1024)S(1)} %pad_clamp_fusion.1), kind=kCustom, calls=%fused_computation | custom fusion | bytes 10486400 | tf_op jit(solution)/shard_map/gather | solution.py:57
  200.2 0.1 multiply_multiply_fusion
  200.3 10.2 %gather_fusion.3 = bf16[160,64,256]{2,1,0:T(8,128)(2,1)} fusion(bf16[160,64,256]{2,1,0:T(8,128)(2,1)} %bitcast.14, s32[1024]{0:T(1024)S(1)} %pad_clamp_fusion.1), kind=kCustom, calls=%fused_computation.3 | custom fusion | bytes 10486400 | tf_op jit(solution)/shard_map/gather | solution.py:57
  210.5 7.4 %fusion.17 = bf16[4,64,336]{2,1,0:T(8,128)(2,1)S(1)} fusion(bf16[4,40,64,256]{3,2,1,0:T(8,128)(2,1)} %bitcast.78, bf16[40,256,336,1]{1,2,0,3:T(8,128)(2,1)} %bitcast.9), kind=kOutput, calls=%fused_computation.32 | convolution fusion | flops 1761693696 | bytes 12296192 | tf_op jit(solution)/shard_map/ksij,sjw->kiw/dot_general | solution.py:91
  217.9 0.1 reshape.171
  218.1 0.3 fusion.13
  218.4 0.3 copy.35
  218.6 0.2 reshape.172
  218.8 7.4 %fusion.16 = bf16[4,64,336]{2,1,0:T(8,128)(2,1)S(1)} fusion(bf16[4,40,64,256]{3,2,1,0:T(8,128)(2,1)} %bitcast.74, bf16[40,256,336,1]{1,2,0,3:T(8,128)(2,1)} %bitcast.9), kind=kOutput, calls=%fused_computation.31 | convolution fusion | flops 1761693696 | bytes 12296192 | tf_op jit(solution)/shard_map/ksij,sjw->kiw/dot_general | solution.py:91
  226.2 0.1 reshape.168
  226.3 0.3 fusion.12
  226.6 0.3 copy.33
  226.9 0.2 reshape.169
  227.1 0.3 fusion.22
  227.4 0.3 convolution_add_fusion.1
  227.8 37.5 %all-to-all-done.1 = bf16[8,5,256,336]{2,3,1,0:T(8,128)(2,1)} async-done(((bf16[8,5,256,336]{2,3,1,0:T(8,128)(2,1)}), bf16[8,5,256,336]{2,3,1,0:T(8,128)(2,1)}, u32[]{:S(2)}, u32[]{:S(2)}) %all-to-all-start.1) | async-done | bytes 6881312 | tf_op jit(solution)/shard_map/all_to_all | solution.py:83
  265.2 7.5 %fusion.19 = bf16[4,64,336]{2,1,0:T(8,128)(2,1)S(1)} fusion(bf16[4,40,64,256]{3,2,1,0:T(8,128)(2,1)} %bitcast.79, bf16[40,256,336,1]{1,2,0,3:T(8,128)(2,1)} %bitcast.21), kind=kOutput, calls=%fused_computation.34 | convolution fusion | flops 1761693696 | bytes 12296192 | tf_op jit(solution)/shard_map/ksij,sjw->kiw/dot_general | solution.py:91
  272.8 5.1 %fusion.18 = bf16[4,64,336]{2,1,0:T(8,128)(2,1)S(1)} fusion(bf16[4,40,64,256]{3,2,1,0:T(8,128)(2,1)S(1)} %bitcast.77, bf16[40,256,336,1]{1,2,0,3:T(8,128)(2,1)} %bitcast.21), kind=kOutput, calls=%fused_computation.33 | convolution fusion | flops 1761693696 | bytes 12296192 | tf_op jit(solution)/shard_map/ksij,sjw->kiw/dot_general | solution.py:91
  277.9 0.1 reshape.176
  278.1 0.3 fusion.15
  278.4 0.3 copy.39
  278.6 0.2 reshape.177
  278.8 0.1 reshape.174
  278.9 0.3 fusion.14
  279.2 0.3 copy.37
  279.5 0.2 reshape.175
  279.7 0.3 fusion.21
  280.0 0.3 convolution_add_fusion
  280.4 0.1 pad_maximum_fusion
  280.5 0.5 copy.40
  280.9 23.4 %all_to_all.15 = f32[8,64,672]{2,1,0:T(8,128)S(1)} all-to-all(f32[8,64,672]{2,1,0:T(8,128)S(1)} %bitcast.72), channel_id=1, replica_groups=mesh['site'=8,'scen'=4] {'site'}, dimensions={0} | all-to-all | bytes 2752512 | tf_op jit(solution)/shard_map/all_to_all | solution.py:107
  304.3 0.1 reduce_sum.45
  304.4 0.1 slice.17
  304.5 3.4 %collective-permute-start.2 = (f32[64,336]{1,0:T(8,128)S(1)}, f32[64,336]{1,0:T(8,128)S(1)}, u32[]{:S(2)}, u32[]{:S(2)}) collective-permute-start(f32[64,336]{1,0:T(8,128)S(1)} %slice.17), channel_id=1, source_target_pairs={{0,2},{1,3},{2,0},{3,1},{4,6},{5,7},{6,4},{7,5},{8,10},{9,11},{10,... | collective-permute-start | bytes 258056 | tf_op jit(solution)/shard_map/ppermute | solution.py:112
  308.0 3.6 %collective-permute-done.2 = f32[64,336]{1,0:T(8,128)S(1)} collective-permute-done((f32[64,336]{1,0:T(8,128)S(1)}, f32[64,336]{1,0:T(8,128)S(1)}, u32[]{:S(2)}, u32[]{:S(2)}) %collective-permute-start.2) | collective-permute-done | bytes 86048 | tf_op jit(solution)/shard_map/ppermute | solution.py:112
  311.6 0.7 slice_add_fusion
  (28 shorter events, 0.3 us)
Async XLA Ops:
  0.0 218.0 %copy-start = (bf16[168,168]{1,0:T(8,128)(2,1)S(1)}, bf16[168,168]{1,0:T(8,128)(2,1)}, u32[]{:S(2)}) copy-start(bf16[168,168]{1,0:T(8,128)(2,1)} %param.10) | copy-start | bytes 169348
  13.8 8.1 %copy-start.1 = (bf16[2560,336]{0,1:T(8,128)(2,1)S(1)}, bf16[2560,336]{0,1:T(8,128)(2,1)}, u32[]{:S(2)}) copy-start(bf16[2560,336]{0,1:T(8,128)(2,1)} %param.7) | copy-start | bytes 5160964
  13.9 168.5 %all-to-all-start = ((bf16[8,5,256,336]{2,3,1,0:T(8,128)(2,1)}), bf16[8,5,256,336]{2,3,1,0:T(8,128)(2,1)}, u32[]{:S(2)}, u32[]{:S(2)}) async-start(bf16[8,5,256,336]{2,3,1,0:T(8,128)(2,1)} %bitcast.69), calls=%async_computation | async-start | bytes 13762560 | tf_op jit(solution)/shard_map/all_to_all | solution.py:83
  19.1 181.2 %collective-permute-start.1 = (bf16[4,40,64,256]{3,2,1,0:T(8,128)(2,1)}, bf16[4,40,64,256]{3,2,1,0:T(8,128)(2,1)}, u32[]{:S(2)}, u32[]{:S(2)}) collective-permute-start(bf16[4,40,64,256]{3,2,1,0:T(8,128)(2,1)} %param.9), channel_id=1, source_target_pairs={{0,1},{1,0},{2,3},{3,2},{4,5},{5,4},{6,7},{7,6},{8,9},{9,8},{10,11... | collective-permute-start | bytes 15728648 | tf_op jit(solution)/shard_map/ppermute | solution.py:22
  21.9 149.9 %collective-permute-start = (bf16[2560,336]{0,1:T(8,128)(2,1)S(1)}, bf16[2560,336]{0,1:T(8,128)(2,1)S(1)}, u32[]{:S(2)}, u32[]{:S(2)}) collective-permute-start(bf16[2560,336]{0,1:T(8,128)(2,1)S(1)} %copy-done.1), channel_id=1, source_target_pairs={{0,2},{1,3},{2,0},{3,1},{4,6},{5,7},{6,4},{7,5},{8,10},{9,11},{10,... | collective-permute-start | bytes 5160968 | tf_op jit(solution)/shard_map/ppermute | solution.py:26
  182.4 6.6 %copy-start.2 = (f32[1024]{0:T(1024)S(1)}, f32[1024]{0:T(1024)}, u32[]{:S(2)}) copy-start(f32[1024]{0:T(1024)} %param.11) | copy-start | bytes 12292
  182.4 6.6 %copy-start.3 = (f32[1024]{0:T(1024)S(1)}, f32[1024]{0:T(1024)}, u32[]{:S(2)}) copy-start(f32[1024]{0:T(1024)} %param.12) | copy-start | bytes 12292
  182.4 82.8 %all-to-all-start.1 = ((bf16[8,5,256,336]{2,3,1,0:T(8,128)(2,1)}), bf16[8,5,256,336]{2,3,1,0:T(8,128)(2,1)}, u32[]{:S(2)}, u32[]{:S(2)}) async-start(bf16[8,5,256,336]{2,3,1,0:T(8,128)(2,1)} %bitcast.68), calls=%async_computation.1 | async-start | bytes 13762560 | tf_op jit(solution)/shard_map/all_to_all | solution.py:83
  227.4 45.4 %slice-start = ((s8[5242880]{0:T(1024)(128)(4,1)}), s8[1048576]{0:T(1024)(128)(4,1)S(1)}, s32[]{:S(2)}) async-start(s8[5242880]{0:T(1024)(128)(4,1)} %bitcast.75), calls=%async_computation.3 | async-start | bytes 2097152
  265.2 7.6 %slice-start.1 = ((s8[5242880]{0:T(1024)(128)(4,1)}), s8[4194304]{0:T(1024)(128)(4,1)S(1)}, s32[]{:S(2)}) async-start(s8[5242880]{0:T(1024)(128)(4,1)} %bitcast.75), calls=%async_computation.4 | async-start | bytes 8388608
  304.5 7.1 %collective-permute-start.2 = (f32[64,336]{1,0:T(8,128)S(1)}, f32[64,336]{1,0:T(8,128)S(1)}, u32[]{:S(2)}, u32[]{:S(2)}) collective-permute-start(f32[64,336]{1,0:T(8,128)S(1)} %slice.17), channel_id=1, source_target_pairs={{0,2},{1,3},{2,0},{3,1},{4,6},{5,7},{6,4},{7,5},{8,10},{9,11},{10,... | collective-permute-start | bytes 258056 | tf_op jit(solution)/shard_map/ppermute | solution.py:112

commit v2 on v1

--- a/solution.py
+++ b/solution.py
@@ -7,6 +7,7 @@
 HOURS = 168
 NZ = 40
 MAX_COLUMN_BLOCKS = 5
+CHUNKS = 2
 
 
 def shards(normals, pattern, factor, temporal, capacity, spread, bus_map, buses):
@@ -19,12 +20,16 @@
     rows_here, _, height, _ = factor.shape
     halves = groups // 2
 
-    partner_factor = lax.ppermute(factor, "scen", [(z, z ^ 1) for z in range(groups)])
     parts = [normals]
     for s in range(1, halves):
-        parts.append(
-            lax.ppermute(normals, "scen", [(z, (z + 2 * s) % groups) for z in range(groups)])
-        )
+        moved = [(z, (z + 2 * s) % groups) for z in range(groups)]
+        parts.append(lax.ppermute(normals, "scen", moved))
+    step = rows_here // CHUNKS
+    partner_chunks = []
+    for c in range(CHUNKS):
+        piece = factor[c * step : (c + 1) * step]
+        swap = [(z, z ^ 1) for z in range(groups)]
+        partner_chunks.append(lax.ppermute(piece, "scen", swap))
 
     block_count = normals.shape[0] // BLK
     all_blocks = block_count * sites
@@ -51,15 +56,19 @@
     place = jnp.sum(jnp.where(match, jnp.arange(NZ, dtype=jnp.int32), 0), axis=2)
     named = jnp.any(match, axis=2)
 
-    def in_slot_order(blocks):
-        flat = blocks.reshape(rows_here * NZ, height, BLK)
-        index = place + jnp.arange(rows_here, dtype=jnp.int32)[:, None] * NZ
-        ordered = flat[index]
+    def in_slot_order(blocks, first):
+        count = blocks.shape[0]
+        flat = blocks.reshape(count * NZ, height, BLK)
+        rows = jnp.arange(count, dtype=jnp.int32)[:, None]
+        ordered = flat[place[first : first + count] + rows * NZ]
         if slots > NZ:
-            ordered = jnp.where(named[:, :, None, None], ordered, jnp.zeros((), flat.dtype))
+            keep = named[first : first + count, :, None, None]
+            ordered = jnp.where(keep, ordered, jnp.zeros((), flat.dtype))
         return ordered
 
-    ordered = [in_slot_order(factor), in_slot_order(partner_factor)]
+    pieces = [(in_slot_order(factor, 0), 0, 0)]
+    for c, chunk in enumerate(partner_chunks):
+        pieces.append((in_slot_order(chunk, c * step), c * step, 1))
 
     starts = [group * height, (group ^ 1) * height]
 
@@ -70,42 +79,41 @@
     scales, spreads = of_rows(capacity), of_rows(spread)
     maps = of_rows(lax.dynamic_slice_in_dim(bus_map, own * rows_here * BLK, rows_here * BLK, 0))
     bus_ids = jnp.arange(buses, dtype=jnp.int32)
-    onehots = [
-        (m.reshape(-1)[None, :] == bus_ids[:, None]).astype(jnp.bfloat16) for m in maps
-    ]
 
     arrivals = []
     for part in parts:
-        outgoing = part.reshape(block_count, BLK, width)[block_index]
+        blocks = part.T.reshape(width, block_count, BLK).transpose(1, 0, 2)
+        outgoing = blocks[block_index]
         if arrivals:
             outgoing, arrivals[-1] = lax.optimization_barrier((outgoing, arrivals[-1]))
-        arrivals.append(
-            lax.all_to_all(outgoing, "site", split_axis=0, concat_axis=0, tiled=True)
-        )
+        arrivals.append(lax.all_to_all(outgoing, "site", split_axis=0, concat_axis=0, tiled=True))
 
     totals = []
     for arrived in arrivals:
-        blocks = arrived.reshape(slots, BLK, width)
+        blocks = arrived.reshape(slots, width, BLK)
         total = None
-        for portion, scale, deviation, onehot in zip(ordered, scales, spreads, onehots):
+        for portion, first, half in pieces:
+            count = portion.shape[0]
             spatial = jnp.einsum(
-                "ksij,sjw->kiw", portion, blocks, preferred_element_type=jnp.float32
+                "ksij,swj->kiw", portion, blocks, preferred_element_type=jnp.float32
             ).astype(jnp.bfloat16)
-            hourly = spatial.reshape(rows_here, height, scen_here, HOURS)
+            hourly = spatial.reshape(count, height, scen_here, HOURS)
             weather = jnp.einsum(
                 "kpsg,hg->kpsh", hourly, temporal, preferred_element_type=jnp.float32
             )
-            scale_part = scale[:, :, None, None]
-            spread_part = deviation[:, :, None, None]
+            scale_part = scales[half][first : first + count, :, None, None]
+            spread_part = spreads[half][first : first + count, :, None, None]
             values = scale_part * jnp.exp(spread_part * weather - 0.5 * spread_part * spread_part)
-            injected = values.astype(jnp.bfloat16).reshape(rows_here * height, width)
+            injected = values.astype(jnp.bfloat16).reshape(count * height, width)
+            here = maps[half][first : first + count].reshape(-1)
+            onehot = (here[None, :] == bus_ids[:, None]).astype(jnp.bfloat16)
             term = jnp.dot(onehot, injected, preferred_element_type=jnp.float32)
             total = term if total is None else total + term
-        totals.append(total)
+        totals.append(total.astype(jnp.bfloat16).reshape(sites, buses // sites, width))
 
-    stacked = jnp.concatenate(totals, axis=1).reshape(sites, buses // sites, -1)
+    stacked = jnp.concatenate(totals, axis=2)
     shares = lax.all_to_all(stacked, "site", split_axis=0, concat_axis=0, tiled=True)
-    mine = jnp.sum(shares, axis=0)
+    mine = jnp.sum(shares.astype(jnp.float32), axis=0)
     result = mine[:, :width]
     for s in range(1, halves):
         back = [(z, (z - 2 * s) % groups) for z in range(groups)]
@@ -119,7 +127,10 @@
 
     def whole(normals, pattern, factor, temporal, capacity, spread, bus_map):
         buses = sites * (factor.shape[0] // sites) * BLK // 16
-        body = lambda *args: shards(*args, buses)
+
+        def body(*args):
+            return shards(*args, buses)
+
         return jax.shard_map(
             body, mesh=mesh, in_specs=placed, out_specs=P("site", "scen"), check_vma=False
         )(normals, pattern, factor, temporal, capacity, spread, bus_map)

time: 313 us -> 253 us (0.81)
  waiting for transfers between devices: 188 us -> 124 us
  matrix products: 29.9 us -> 40.3 us
  blocking collectives: 23.4 us -> 16.2 us
    all_to_all x2, waiting for transfers between devices: 37.5 us -> 0.01 us  [shards(): lax.all_to_all(outgoing, 'site', split_axis=0, concat_axis=0, tiled=True)]
    ppermute x2 -> x3, waiting for transfers between devices: 147 us -> 118 us  [the longest x1 65.4 us: shards(): parts.append(lax.ppermute(normals, 'scen', moved))]
    dot_general x4 -> x6, matrix products: 27.4 us -> 37 us  [shards(): jnp.einsum('ksij,swj->kiw', portion, blocks, preferred_element_type=jnp.f...]
    all_to_all x1, blocking collectives: 23.4 us -> 16.2 us  [shards(): lax.all_to_all(stacked, 'site', split_axis=0, concat_axis=0, tiled=True)]
    transpose x0 -> x2, local copies, waits for them, and re-layouts: none -> 6.37 us  [shards(): blocks = part.T.reshape(width, block_count, BLK).transpose(1, 0, 2)]
    slice x0 -> x3, local copies, waits for them, and re-layouts: none -> 5.72 us  [the longest x1 5.71 us: shards(): piece = factor[c * step:(c + 1) * step]]
    unnamed x13 -> x10, local copies, waits for them, and re-layouts: 3.92 us -> 0.02 us
    gather x4 -> x5, local copies, waits for them, and re-layouts: 31.3 us -> 27.6 us  [the longest x3 16.9 us: in_slot_order(): ordered = flat[place[first:first + count] + rows * NZ]]
  transfers between devices with their start and end apart: 5 -> 6, of which waited for: 3 -> 3; matrix products, arithmetic and copies ran while one was open for 16% -> 23% of each run, Pallas kernels for 0% -> 0%
where the time goes in v2:
time: 253 us; the launch traced here: 252 us
  waiting for transfers between devices  124 us (49%)
  local copies, waits for them, and re-layouts  51.7 us (20%)
  matrix products  40.3 us (16%)
  starting transfers between devices  16.6 us (7%)
  blocking collectives  16.2 us (6%)
  other arithmetic  2.58 us (1%)
    ppermute x1, waiting for transfers between devices, shards(): parts.append(lax.ppermute(normals, 'scen', moved))  65.4 us
    ppermute x2, waiting for transfers between devices, shards(): partner_chunks.append(lax.ppermute(piece, 'scen', swap))  52.2 us
    dot_general x6, matrix products, shards(): jnp.einsum('ksij,swj->kiw', portion, blocks, preferred_element_type=jnp.f...  37 us
    gather x3, local copies, waits for them, and re-layouts, in_slot_order(): ordered = flat[place[first:first + count] + rows * NZ]  16.9 us
    all_to_all x1, blocking collectives, shards(): lax.all_to_all(stacked, 'site', split_axis=0, concat_axis=0, tiled=True)  16.2 us
    gather x2, local copies, waits for them, and re-layouts, shards(): outgoing = blocks[block_index]  10.8 us
    all_to_all x2, starting transfers between devices, shards(): lax.all_to_all(outgoing, 'site', split_axis=0, concat_axis=0, tiled=True)  10.3 us
    transpose x2, local copies, waits for them, and re-layouts, shards(): blocks = part.T.reshape(width, block_count, BLK).transpose(1, 0, 2)  6.37 us
  transfers between devices with their start and end apart: 6, of which 3 were waited for; matrix products, arithmetic and copies ran while one was open for 23% of the time, Pallas kernels for 0%

profile of v2, /device:TPU:0, one launch (start us, length us, event | category | flops | bytes accessed | tf_op | source)
XLA Modules:
  0.0 251.7 jit_solution(1885378691643352239)
XLA Ops:
  0.0 0.8 eq.62
  0.8 0.3 fusion.32
  1.2 0.2 reduce_window_sum.18
  1.3 0.2 select_reduce_fusion.2
  1.7 3.9 %copy.37 = bf16[336,2560]{0,1:T(8,128)(2,1)} copy(bf16[336,2560]{1,0:T(8,128)(2,1)} %bitcast.108) | data formatting | bytes 3440640 | tf_op jit(solution)/shard_map/transpose | solution.py:85
  5.6 2.8 %copy.38 = bf16[336,10,256]{2,0,1:T(8,128)(2,1)S(1)} copy(bf16[336,10,256]{0,2,1:T(8,128)(2,1)} %bitcast.105) | data formatting | bytes 3440640 | tf_op jit(solution)/shard_map/reshape | solution.py:85
  8.4 5.4 %gather_fusion.2 = bf16[40,336,256]{2,1,0:T(8,128)(2,1)} fusion(bf16[10,336,256]{2,1,0:T(8,128)(2,1)S(1)} %bitcast.100, s32[1024]{0:T(1024)S(1)} %pad_clamp_fusion.2), kind=kCustom, calls=%fused_computation.2 | custom fusion | bytes 13762720 | tf_op jit(solution)/shard_map/gather | solution.py:86
  13.8 5.4 %all-to-all-start = ((bf16[8,5,336,256]{3,2,1,0:T(8,128)(2,1)}), bf16[8,5,336,256]{3,2,1,0:T(8,128)(2,1)}, u32[]{:S(2)}, u32[]{:S(2)}) async-start(bf16[8,5,336,256]{3,2,1,0:T(8,128)(2,1)} %bitcast.102), calls=%async_computation | async-start | bytes 13762560 | tf_op jit(solution)/shard_map/all_to_all | solution.py:89
  19.2 3.7 %collective-permute-start = (bf16[2560,336]{0,1:T(8,128)(2,1)S(1)}, bf16[2560,336]{0,1:T(8,128)(2,1)S(1)}, u32[]{:S(2)}, u32[]{:S(2)}) collective-permute-start(bf16[2560,336]{0,1:T(8,128)(2,1)S(1)} %copy-done.2), channel_id=1, source_target_pairs={{0,2},{1,3},{2,0},{3,1},{4,6},{5,7},{6,4},{7,5},{8,10},{9,11},{10,... | collective-permute-start | bytes 5160968 | tf_op jit(solution)/shard_map/ppermute | solution.py:26
  22.9 5.7 %fusion.58 = (bf16[2,40,64,256]{3,2,1,0:T(8,128)(2,1)}, bf16[2,40,64,256]{3,2,1,0:T(8,128)(2,1)}) fusion(bf16[4,40,64,256]{3,2,1,0:T(8,128)(2,1)} %param.9), kind=kLoop, calls=%fused_computation.122 | loop fusion | bytes 10485760 | tf_op jit(solution)/shard_map/slice | solution.py:30
  28.6 1.6 collective-permute-start.2
  30.2 0.4 collective-permute-start.1
  30.6 0.7 dynamic_slice.31
  31.4 0.2 reduce_window_sum.17
  31.7 0.7 constant_dynamic-slice_fusion.4
  32.5 65.4 %collective-permute-done = bf16[2560,336]{0,1:T(8,128)(2,1)S(1)} collective-permute-done((bf16[2560,336]{0,1:T(8,128)(2,1)S(1)}, bf16[2560,336]{0,1:T(8,128)(2,1)S(1)}, u32[]{:S(2)}, u32[]{:S(2)}) %collective-permute-start) | collective-permute-done | bytes 1720352 | tf_op jit(solution)/shard_map/ppermute | solution.py:26
  97.9 2.5 copy.34
  100.4 2.8 %copy.35 = bf16[336,10,256]{2,0,1:T(8,128)(2,1)S(1)} copy(bf16[336,10,256]{0,2,1:T(8,128)(2,1)} %bitcast.104) | data formatting | bytes 3440640 | tf_op jit(solution)/shard_map/reshape | solution.py:85
  103.2 5.3 %gather_fusion.1 = bf16[40,336,256]{2,1,0:T(8,128)(2,1)} fusion(bf16[10,336,256]{2,1,0:T(8,128)(2,1)S(1)} %bitcast.99, s32[1024]{0:T(1024)S(1)} %pad_clamp_fusion.2), kind=kCustom, calls=%fused_computation.1 | custom fusion | bytes 13762720 | tf_op jit(solution)/shard_map/gather | solution.py:86
  108.5 4.9 %all-to-all-start.1 = ((bf16[8,5,336,256]{3,2,1,0:T(8,128)(2,1)}), bf16[8,5,336,256]{3,2,1,0:T(8,128)(2,1)}, u32[]{:S(2)}, u32[]{:S(2)}) async-start(bf16[8,5,336,256]{3,2,1,0:T(8,128)(2,1)} %bitcast.101), calls=%async_computation.1 | async-start | bytes 13762560 | tf_op jit(solution)/shard_map/all_to_all | solution.py:89
  113.7 0.2 select_reduce_fusion.1
  114.0 0.2 select_reduce_fusion
  114.5 10.2 %gather_fusion = bf16[160,64,256]{2,1,0:T(8,128)(2,1)} fusion(bf16[160,64,256]{2,1,0:T(8,128)(2,1)} %bitcast.103, s32[1024]{0:T(1024)S(1)} %pad_clamp_fusion.3), kind=kCustom, calls=%fused_computation | custom fusion | bytes 10486400 | tf_op jit(solution)/shard_map/gather | solution.py:63
  124.9 2.5 gather_fusion.4
  127.4 52.2 %collective-permute-done.1 = bf16[2,40,64,256]{3,2,1,0:T(8,128)(2,1)} collective-permute-done((bf16[2,40,64,256]{3,2,1,0:T(8,128)(2,1)}, bf16[2,40,64,256]{3,2,1,0:T(8,128)(2,1)}, u32[]{:S(2)}, u32[]{:S(2)}) %collective-permute-start.1) | collective-permute-done | bytes 2621472 | tf_op jit(solution)/shard_map/ppermute | solution.py:32
  179.6 4.1 %gather_fusion.3 = bf16[80,64,256]{2,1,0:T(8,128)(2,1)} fusion(bf16[80,64,256]{2,1,0:T(8,128)(2,1)} %bitcast.18, s32[1024]{0:T(1024)S(1)} %pad_clamp_fusion.1), kind=kCustom, calls=%fused_computation.3 | custom fusion | bytes 5243200 | tf_op jit(solution)/shard_map/gather | solution.py:63
  183.7 7.4 %fusion.10 = bf16[4,64,336]{2,1,0:T(8,128)(2,1)S(1)} fusion(bf16[4,40,64,256]{3,2,1,0:T(8,128)(2,1)} %bitcast.106, bf16[40,336,256,1]{2,1,0,3:T(8,128)(2,1)} %bitcast.13), kind=kOutput, calls=%fused_computation.24 | convolution fusion | flops 1761693696 | bytes 12296192 | tf_op jit(solution)/shard_map/ksij,swj->kiw/dot_general | solution.py:97
  191.1 0.1 reshape.197
  191.3 0.3 fusion.8
  191.6 0.3 copy.40
  191.9 0.2 reshape.198
  192.0 5.3 %fusion.29 = bf16[2,64,336]{2,1,0:T(8,128)(2,1)S(1)} fusion(bf16[2,40,64,256]{3,2,1,0:T(8,128)(2,1)S(1)} %bitcast.95, bf16[40,336,256,1]{2,1,0,3:T(8,128)(2,1)} %bitcast.13), kind=kOutput, calls=%fused_computation.51 | convolution fusion | flops 880846848 | bytes 9588736 | tf_op jit(solution)/shard_map/ksij,swj->kiw/dot_general | solution.py:97
  197.5 0.2 fusion.25
  197.7 0.1 copy.44
  197.8 0.1 reshape.204
  198.0 6.1 %fusion.28 = bf16[2,64,336]{2,1,0:T(8,128)(2,1)S(1)} fusion(bf16[2,40,64,256]{3,2,1,0:T(8,128)(2,1)} %bitcast.97, bf16[40,336,256,1]{2,1,0,3:T(8,128)(2,1)} %bitcast.13), kind=kOutput, calls=%fused_computation.50 | convolution fusion | flops 880846848 | bytes 9588736 | tf_op jit(solution)/shard_map/ksij,swj->kiw/dot_general | solution.py:97
  204.2 0.2 fusion.24
  204.4 0.1 copy.42
  204.5 0.1 reshape.201
  204.7 0.3 fusion.34
  205.0 0.3 convolution_add_fusion.3
  205.3 0.3 fusion.6
  205.6 0.2 copy.45
  205.8 7.4 %fusion.11 = bf16[4,64,336]{2,1,0:T(8,128)(2,1)S(1)} fusion(bf16[4,40,64,256]{3,2,1,0:T(8,128)(2,1)} %bitcast.107, bf16[40,336,256,1]{2,1,0,3:T(8,128)(2,1)} %bitcast.30), kind=kOutput, calls=%fused_computation.25 | convolution fusion | flops 1761693696 | bytes 12296192 | tf_op jit(solution)/shard_map/ksij,swj->kiw/dot_general | solution.py:97
  213.2 5.5 %fusion.31 = bf16[2,64,336]{2,1,0:T(8,128)(2,1)S(1)} fusion(bf16[2,40,64,256]{3,2,1,0:T(8,128)(2,1)S(1)} %bitcast.96, bf16[40,336,256,1]{2,1,0,3:T(8,128)(2,1)} %bitcast.30), kind=kOutput, calls=%fused_computation.53 | convolution fusion | flops 880846848 | bytes 9588736 | tf_op jit(solution)/shard_map/ksij,swj->kiw/dot_general | solution.py:97
  218.7 5.3 %fusion.30 = bf16[2,64,336]{2,1,0:T(8,128)(2,1)S(1)} fusion(bf16[2,40,64,256]{3,2,1,0:T(8,128)(2,1)S(1)} %bitcast.98, bf16[40,336,256,1]{2,1,0,3:T(8,128)(2,1)} %bitcast.30), kind=kOutput, calls=%fused_computation.52 | convolution fusion | flops 880846848 | bytes 9588736 | tf_op jit(solution)/shard_map/ksij,swj->kiw/dot_general | solution.py:97
  224.0 0.1 reshape.207
  224.2 0.3 fusion.9
  224.5 0.5 copy.47
  225.0 0.2 reshape.208
  225.1 0.3 fusion.33
  225.6 0.2 fusion.27
  225.8 0.1 copy.51
  226.0 0.1 reshape.212
  226.2 0.2 fusion.26
  226.4 0.1 copy.49
  226.7 0.3 convolution_add_fusion.1
  227.0 0.3 fusion.7
  227.3 0.2 copy.52
  227.5 0.3 pad_maximum_fusion
  227.8 16.2 %all_to_all.15 = bf16[8,64,672]{2,1,0:T(8,128)(2,1)S(1)} all-to-all(bf16[8,64,672]{2,1,0:T(8,128)(2,1)S(1)} %pad_maximum_fusion), channel_id=1, replica_groups=mesh['site'=8,'scen'=4] {'site'}, dimensions={0} | all-to-all | bytes 1376256 | tf_op jit(solution)/shard_map/all_to_all | solution.py:115
  244.2 0.5 collective-permute-start.3
  244.7 6.3 %collective-permute-done.3 = f32[64,336]{1,0:T(8,128)S(1)} collective-permute-done((f32[64,336]{1,0:T(8,128)S(1)}, f32[64,336]{1,0:T(8,128)S(1)}, u32[]{:S(2)}, u32[]{:S(2)}) %collective-permute-start.3) | collective-permute-done | bytes 86048 | tf_op jit(solution)/shard_map/ppermute | solution.py:120
  251.0 0.7 slice_add_fusion
  (52 shorter events, 2.1 us)
Async XLA Ops:
  0.0 191.3 %copy-start = (bf16[168,168]{1,0:T(8,128)(2,1)S(1)}, bf16[168,168]{1,0:T(8,128)(2,1)}, u32[]{:S(2)}) copy-start(bf16[168,168]{1,0:T(8,128)(2,1)} %param.10) | copy-start | bytes 169348
  13.8 5.4 %copy-start.2 = (bf16[2560,336]{0,1:T(8,128)(2,1)S(1)}, bf16[2560,336]{0,1:T(8,128)(2,1)}, u32[]{:S(2)}) copy-start(bf16[2560,336]{0,1:T(8,128)(2,1)} %param.7) | copy-start | bytes 5160964
  13.8 94.7 %all-to-all-start = ((bf16[8,5,336,256]{3,2,1,0:T(8,128)(2,1)}), bf16[8,5,336,256]{3,2,1,0:T(8,128)(2,1)}, u32[]{:S(2)}, u32[]{:S(2)}) async-start(bf16[8,5,336,256]{3,2,1,0:T(8,128)(2,1)} %bitcast.102), calls=%async_computation | async-start | bytes 13762560 | tf_op jit(solution)/shard_map/all_to_all | solution.py:89
  19.2 78.7 %collective-permute-start = (bf16[2560,336]{0,1:T(8,128)(2,1)S(1)}, bf16[2560,336]{0,1:T(8,128)(2,1)S(1)}, u32[]{:S(2)}, u32[]{:S(2)}) collective-permute-start(bf16[2560,336]{0,1:T(8,128)(2,1)S(1)} %copy-done.2), channel_id=1, source_target_pairs={{0,2},{1,3},{2,0},{3,1},{4,6},{5,7},{6,4},{7,5},{8,10},{9,11},{10,... | collective-permute-start | bytes 5160968 | tf_op jit(solution)/shard_map/ppermute | solution.py:26
  28.6 96.3 %collective-permute-start.2 = (bf16[2,40,64,256]{3,2,1,0:T(8,128)(2,1)}, bf16[2,40,64,256]{3,2,1,0:T(8,128)(2,1)}, u32[]{:S(2)}, u32[]{:S(2)}) collective-permute-start(bf16[2,40,64,256]{3,2,1,0:T(8,128)(2,1)} %get-tuple-element.11), channel_id=1, source_target_pairs={{0,1},{1,0},{2,3},{3,2},{4,5},{5,4},{6,7},{7,6},{8,9},{9,8},{10,11... | collective-permute-start | bytes 7864328 | tf_op jit(solution)/shard_map/ppermute | solution.py:32
  30.2 149.4 %collective-permute-start.1 = (bf16[2,40,64,256]{3,2,1,0:T(8,128)(2,1)}, bf16[2,40,64,256]{3,2,1,0:T(8,128)(2,1)}, u32[]{:S(2)}, u32[]{:S(2)}) collective-permute-start(bf16[2,40,64,256]{3,2,1,0:T(8,128)(2,1)} %get-tuple-element.12), channel_id=1, source_target_pairs={{0,1},{1,0},{2,3},{3,2},{4,5},{5,4},{6,7},{7,6},{8,9},{9,8},{10,11... | collective-permute-start | bytes 7864328 | tf_op jit(solution)/shard_map/ppermute | solution.py:32
  108.5 5.2 %copy-start.3 = (f32[1024]{0:T(1024)S(1)}, f32[1024]{0:T(1024)}, u32[]{:S(2)}) copy-start(f32[1024]{0:T(1024)} %param.11) | copy-start | bytes 12292
  108.5 5.2 %copy-start.4 = (f32[1024]{0:T(1024)S(1)}, f32[1024]{0:T(1024)}, u32[]{:S(2)}) copy-start(f32[1024]{0:T(1024)} %param.12) | copy-start | bytes 12292
  108.5 97.3 %all-to-all-start.1 = ((bf16[8,5,336,256]{3,2,1,0:T(8,128)(2,1)}), bf16[8,5,336,256]{3,2,1,0:T(8,128)(2,1)}, u32[]{:S(2)}, u32[]{:S(2)}) async-start(bf16[8,5,336,256]{3,2,1,0:T(8,128)(2,1)} %bitcast.101), calls=%async_computation.1 | async-start | bytes 13762560 | tf_op jit(solution)/shard_map/all_to_all | solution.py:89
  213.2 5.5 %copy-start.1 = (bf16[80,64,256]{2,1,0:T(8,128)(2,1)S(1)}, bf16[80,64,256]{2,1,0:T(8,128)(2,1)}, u32[]{:S(2)}) copy-start(bf16[80,64,256]{2,1,0:T(8,128)(2,1)} %gather_fusion.3) | copy-start | bytes 7864324
  244.2 6.8 %collective-permute-start.3 = (f32[64,336]{1,0:T(8,128)S(1)}, f32[64,336]{1,0:T(8,128)S(1)}, u32[]{:S(2)}, u32[]{:S(2)}) collective-permute-start(f32[64,336]{1,0:T(8,128)S(1)} %slice.65), channel_id=1, source_target_pairs={{0,2},{1,3},{2,0},{3,1},{4,6},{5,7},{6,4},{7,5},{8,10},{9,11},{10,... | collective-permute-start | bytes 258056 | tf_op jit(solution)/shard_map/ppermute | solution.py:120

commit v3 on v2

--- a/solution.py
+++ b/solution.py
@@ -1,13 +1,40 @@
 import jax
 import jax.numpy as jnp
 from jax import lax
+from jax.experimental import pallas as pl
+from jax.experimental.pallas import tpu as pltpu
 from jax.sharding import PartitionSpec as P
 
 BLK = 256
 HOURS = 168
 NZ = 40
 MAX_COLUMN_BLOCKS = 5
-CHUNKS = 2
+CHUNKS = 1
+
+
+def pick_body(index_ref, table_ref, out_ref):
+    row = pl.program_id(0)
+    for slot in range(MAX_COLUMN_BLOCKS):
+        start = pl.multiple_of(index_ref[row, slot] * BLK, BLK)
+        out_ref[0, slot] = table_ref[:, pl.ds(start, BLK)]
+
+
+def pick(index, table):
+    sites, slots = index.shape
+    width, lanes = table.shape
+    return pl.pallas_call(
+        pick_body,
+        grid_spec=pltpu.PrefetchScalarGridSpec(
+            num_scalar_prefetch=1,
+            grid=(sites,),
+            in_specs=[pl.BlockSpec((width, lanes), lambda i, index_ref: (0, 0))],
+            out_specs=pl.BlockSpec((1, slots, width, BLK), lambda i, index_ref: (i, 0, 0, 0)),
+        ),
+        out_shape=jax.ShapeDtypeStruct((sites, slots, width, BLK), table.dtype),
+        cost_estimate=pl.CostEstimate(
+            flops=0, bytes_accessed=2 * sites * slots * width * BLK * 2, transcendentals=0
+        ),
+    )(index, table)
 
 
 def shards(normals, pattern, factor, temporal, capacity, spread, bus_map, buses):
@@ -27,7 +54,7 @@
     step = rows_here // CHUNKS
     partner_chunks = []
     for c in range(CHUNKS):
-        piece = factor[c * step : (c + 1) * step]
+        piece = factor[c * step : (c + 1) * step] if CHUNKS > 1 else factor
         swap = [(z, z ^ 1) for z in range(groups)]
         partner_chunks.append(lax.ppermute(piece, "scen", swap))
 
@@ -82,8 +109,7 @@
 
     arrivals = []
     for part in parts:
-        blocks = part.T.reshape(width, block_count, BLK).transpose(1, 0, 2)
-        outgoing = blocks[block_index]
+        outgoing = pick(block_index, part.T)
         if arrivals:
             outgoing, arrivals[-1] = lax.optimization_barrier((outgoing, arrivals[-1]))
         arrivals.append(lax.all_to_all(outgoing, "site", split_axis=0, concat_axis=0, tiled=True))

time: 253 us -> 296 us (1.17)
  waiting for transfers between devices: 124 us -> 188 us
  local copies, waits for them, and re-layouts: 51.7 us -> 27.9 us
  Pallas kernels: 0 us -> 12.9 us
  matrix products: 40.3 us -> 29.9 us
    ppermute x1, waiting for transfers between devices: 65.4 us -> 147 us  [shards(): parts.append(lax.ppermute(normals, 'scen', moved))]
    ppermute x2 -> x1, waiting for transfers between devices: 52.2 us -> 0.01 us  [shards(): partner_chunks.append(lax.ppermute(piece, 'scen', swap))]
    all_to_all x2, waiting for transfers between devices: 0.01 us -> 37.3 us  [shards(): lax.all_to_all(outgoing, 'site', split_axis=0, concat_axis=0, tiled=True)]
    pallas_call x0 -> x2, Pallas kernels: none -> 12.9 us  [pick(): pl.pallas_call(pick_body, grid_spec=pltpu.PrefetchScalarGridSpec(num_scal...]
    gather x2 -> x0, local copies, waits for them, and re-layouts: 10.8 us -> none  [shards(): outgoing = blocks[block_index]]
    dot_general x6 -> x4, matrix products: 37 us -> 27.4 us  [shards(): jnp.einsum('ksij,swj->kiw', portion, blocks, preferred_element_type=jnp.f...]
    transpose x2 -> x0, local copies, waits for them, and re-layouts: 6.37 us -> none  [shards(): blocks = part.T.reshape(width, block_count, BLK).transpose(1, 0, 2)]
    slice x3 -> x0, local copies, waits for them, and re-layouts: 5.72 us -> none  [the longest x1 5.71 us: shards(): piece = factor[c * step:(c + 1) * step]]
  transfers between devices with their start and end apart: 6 -> 5, of which waited for: 3 -> 3; matrix products, arithmetic and copies ran while one was open for 23% -> 14% of each run, Pallas kernels for 0% -> 2%
where the time goes in v3:
time: 296 us
  waiting for transfers between devices  188 us (64%)
  matrix products  29.9 us (10%)
  local copies, waits for them, and re-layouts  27.9 us (9%)
  starting transfers between devices  19 us (6%)
  blocking collectives  14.9 us (5%)
  Pallas kernels  12.9 us (4%)
    ppermute x1, waiting for transfers between devices, shards(): parts.append(lax.ppermute(normals, 'scen', moved))  147 us
    all_to_all x2, waiting for transfers between devices, shards(): lax.all_to_all(outgoing, 'site', split_axis=0, concat_axis=0, tiled=True)  37.3 us
    dot_general x4, matrix products, shards(): jnp.einsum('ksij,swj->kiw', portion, blocks, preferred_element_type=jnp.f...  27.4 us
    gather x2, local copies, waits for them, and re-layouts, in_slot_order(): ordered = flat[place[first:first + count] + rows * NZ]  20.5 us
    all_to_all x1, blocking collectives, shards(): lax.all_to_all(stacked, 'site', split_axis=0, concat_axis=0, tiled=True)  14.9 us
    pallas_call x2, Pallas kernels, pick(): pl.pallas_call(pick_body, grid_spec=pltpu.PrefetchScalarGridSpec(num_scal...  12.9 us
    all_to_all x2, starting transfers between devices, shards(): lax.all_to_all(outgoing, 'site', split_axis=0, concat_axis=0, tiled=True)  10.3 us
  transfers between devices with their start and end apart: 5, of which 3 were waited for; matrix products, arithmetic and copies ran while one was open for 14% of the time, Pallas kernels for 2%

profile of v3, /device:TPU:0, one launch (start us, length us, event | category | flops | bytes accessed | tf_op | source)
XLA Modules:
  0.0 295.6 jit_solution(12635798804601380767)
XLA Ops:
  0.0 0.8 eq.54
  0.8 0.3 fusion.22
  1.1 0.1 broadcast_compare_fusion
  1.2 0.2 reduce_window_sum.18
  1.3 0.2 select_reduce_fusion.2
  1.5 0.7 copy.22.index_ref
  2.2 6.5 %shard_map.74 = bf16[8,5,336,256]{3,2,1,0:T(8,128)(2,1)} custom-call(s32[8,5]{1,0:T(8,128)} %copy.22.index_ref, bf16[336,2560]{1,0:T(8,128)(2,1)} %bitcast.70), custom_call_target="tpu_custom_call" | custom-call | bytes 13762560 | tf_op jit(solution)/shard_map/pallas_call | solution.py:25
  8.7 5.3 %all-to-all-start = ((bf16[8,5,336,256]{3,2,1,0:T(8,128)(2,1)}), bf16[8,5,336,256]{3,2,1,0:T(8,128)(2,1)}, u32[]{:S(2)}, u32[]{:S(2)}) async-start(bf16[8,5,336,256]{3,2,1,0:T(8,128)(2,1)} %shard_map.74), calls=%async_computation | async-start | bytes 13762560 | tf_op jit(solution)/shard_map/all_to_all | solution.py:115
  14.0 2.7 collective-permute-start.1
  16.8 2.6 collective-permute-start
  19.4 147.3 %collective-permute-done = bf16[2560,336]{0,1:T(8,128)(2,1)S(1)} collective-permute-done((bf16[2560,336]{0,1:T(8,128)(2,1)S(1)}, bf16[2560,336]{0,1:T(8,128)(2,1)S(1)}, u32[]{:S(2)}, u32[]{:S(2)}) %collective-permute-start) | collective-permute-done | bytes 1720352 | tf_op jit(solution)/shard_map/ppermute | solution.py:53
  166.6 1.2 copy-done.2
  167.8 6.4 %shard_map.73 = bf16[8,5,336,256]{3,2,1,0:T(8,128)(2,1)} custom-call(s32[8,5]{1,0:T(8,128)} %copy.22.index_ref, bf16[336,2560]{1,0:T(8,128)(2,1)} %bitcast.71), custom_call_target="tpu_custom_call" | custom-call | bytes 13762560 | tf_op jit(solution)/shard_map/pallas_call | solution.py:25
  174.3 4.9 %all-to-all-start.1 = ((bf16[8,5,336,256]{3,2,1,0:T(8,128)(2,1)}), bf16[8,5,336,256]{3,2,1,0:T(8,128)(2,1)}, u32[]{:S(2)}, u32[]{:S(2)}) async-start(bf16[8,5,336,256]{3,2,1,0:T(8,128)(2,1)} %shard_map.73), calls=%async_computation.1 | async-start | bytes 13762560 | tf_op jit(solution)/shard_map/all_to_all | solution.py:115
  179.2 0.1 reshape.162
  179.3 0.2 reduce_window_sum.17
  179.5 0.1 sub.44
  179.6 0.7 constant_dynamic-slice_fusion.4
  180.3 0.2 select_reduce_fusion.1
  180.5 0.2 select_reduce_fusion
  180.7 0.1 compare_select_fusion
  180.7 0.1 reshape.165
  180.9 0.7 dynamic_slice.31
  181.6 0.1 constant_dynamic-slice_fusion
  181.6 0.1 eq.47
  181.7 0.1 eq.124
  181.8 10.3 %gather_fusion = bf16[160,64,256]{2,1,0:T(8,128)(2,1)} fusion(bf16[160,64,256]{2,1,0:T(8,128)(2,1)} %bitcast.63, s32[1024]{0:T(1024)S(1)} %pad_clamp_fusion), kind=kCustom, calls=%fused_computation | custom fusion | bytes 10486400 | tf_op jit(solution)/shard_map/gather | solution.py:90
  192.1 0.1 multiply_multiply_fusion
  192.1 0.0 collective-permute-done.1
  192.2 10.2 %gather_fusion.1 = bf16[160,64,256]{2,1,0:T(8,128)(2,1)} fusion(bf16[160,64,256]{2,1,0:T(8,128)(2,1)} %bitcast.11, s32[1024]{0:T(1024)S(1)} %pad_clamp_fusion), kind=kCustom, calls=%fused_computation.1 | custom fusion | bytes 10486400 | tf_op jit(solution)/shard_map/gather | solution.py:90
  202.4 7.4 %fusion.19 = bf16[4,64,336]{2,1,0:T(8,128)(2,1)S(1)} fusion(bf16[4,40,64,256]{3,2,1,0:T(8,128)(2,1)} %bitcast.68, bf16[40,336,256,1]{2,1,0,3:T(8,128)(2,1)} %bitcast.6), kind=kOutput, calls=%fused_computation.32 | convolution fusion | flops 1761693696 | bytes 12296192 | tf_op jit(solution)/shard_map/ksij,swj->kiw/dot_general | solution.py:123
  209.8 0.1 reshape.153
  209.9 0.3 fusion.15
  210.2 0.3 copy.27
  210.5 0.2 reshape.154
  210.7 7.4 %fusion.18 = bf16[4,64,336]{2,1,0:T(8,128)(2,1)S(1)} fusion(bf16[4,40,64,256]{3,2,1,0:T(8,128)(2,1)} %bitcast.64, bf16[40,336,256,1]{2,1,0,3:T(8,128)(2,1)} %bitcast.6), kind=kOutput, calls=%fused_computation.31 | convolution fusion | flops 1761693696 | bytes 12296192 | tf_op jit(solution)/shard_map/ksij,swj->kiw/dot_general | solution.py:123
  218.1 0.1 reshape.150
  218.2 0.3 fusion.14
  218.5 0.3 copy.25
  218.8 0.2 reshape.151
  218.9 0.3 fusion.24
  219.3 0.3 fusion.12
  219.6 0.2 copy.28
  219.8 37.3 %all-to-all-done.1 = bf16[8,5,336,256]{3,2,1,0:T(8,128)(2,1)} async-done(((bf16[8,5,336,256]{3,2,1,0:T(8,128)(2,1)}), bf16[8,5,336,256]{3,2,1,0:T(8,128)(2,1)}, u32[]{:S(2)}, u32[]{:S(2)}) %all-to-all-start.1) | async-done | bytes 6881312 | tf_op jit(solution)/shard_map/all_to_all | solution.py:115
  257.1 7.5 %fusion.21 = bf16[4,64,336]{2,1,0:T(8,128)(2,1)S(1)} fusion(bf16[4,40,64,256]{3,2,1,0:T(8,128)(2,1)} %bitcast.69, bf16[40,336,256,1]{2,1,0,3:T(8,128)(2,1)} %bitcast.19), kind=kOutput, calls=%fused_computation.34 | convolution fusion | flops 1761693696 | bytes 12296192 | tf_op jit(solution)/shard_map/ksij,swj->kiw/dot_general | solution.py:123
  264.7 5.1 %fusion.20 = bf16[4,64,336]{2,1,0:T(8,128)(2,1)S(1)} fusion(bf16[4,40,64,256]{3,2,1,0:T(8,128)(2,1)S(1)} %bitcast.67, bf16[40,336,256,1]{2,1,0,3:T(8,128)(2,1)} %bitcast.19), kind=kOutput, calls=%fused_computation.33 | convolution fusion | flops 1761693696 | bytes 12296192 | tf_op jit(solution)/shard_map/ksij,swj->kiw/dot_general | solution.py:123
  269.8 0.1 reshape.159
  269.9 0.3 fusion.17
  270.2 0.3 copy.32
  270.5 0.2 reshape.160
  270.7 0.1 reshape.157
  270.8 0.3 fusion.16
  271.1 0.3 copy.30
  271.4 0.2 reshape.158
  271.5 0.3 fusion.23
  271.9 0.3 fusion.13
  272.2 0.2 copy.33
  272.4 0.3 pad_maximum_fusion
  272.7 14.9 %all_to_all.15 = bf16[8,64,672]{2,1,0:T(8,128)(2,1)S(1)} all-to-all(bf16[8,64,672]{2,1,0:T(8,128)(2,1)S(1)} %pad_maximum_fusion), channel_id=1, replica_groups=mesh['site'=8,'scen'=4] {'site'}, dimensions={0} | all-to-all | bytes 1376256 | tf_op jit(solution)/shard_map/all_to_all | solution.py:141
  287.7 0.1 convert_reduce_fusion
  287.8 0.1 slice.13
  287.9 3.4 %collective-permute-start.2 = (f32[64,336]{1,0:T(8,128)S(1)}, f32[64,336]{1,0:T(8,128)S(1)}, u32[]{:S(2)}, u32[]{:S(2)}) collective-permute-start(f32[64,336]{1,0:T(8,128)S(1)} %slice.13), channel_id=1, source_target_pairs={{0,2},{1,3},{2,0},{3,1},{4,6},{5,7},{6,4},{7,5},{8,10},{9,11},{10,... | collective-permute-start | bytes 258056 | tf_op jit(solution)/shard_map/ppermute | solution.py:146
  291.3 3.6 %collective-permute-done.2 = f32[64,336]{1,0:T(8,128)S(1)} collective-permute-done((f32[64,336]{1,0:T(8,128)S(1)}, f32[64,336]{1,0:T(8,128)S(1)}, u32[]{:S(2)}, u32[]{:S(2)}) %collective-permute-start.2) | collective-permute-done | bytes 86048 | tf_op jit(solution)/shard_map/ppermute | solution.py:146
  295.0 0.7 slice_add_fusion
  (24 shorter events, 0.1 us)
Async XLA Ops:
  0.0 209.9 %copy-start = (bf16[168,168]{1,0:T(8,128)(2,1)S(1)}, bf16[168,168]{1,0:T(8,128)(2,1)}, u32[]{:S(2)}) copy-start(bf16[168,168]{1,0:T(8,128)(2,1)} %param.10) | copy-start | bytes 169348
  8.7 8.1 %copy-start.1 = (bf16[2560,336]{0,1:T(8,128)(2,1)S(1)}, bf16[2560,336]{0,1:T(8,128)(2,1)}, u32[]{:S(2)}) copy-start(bf16[2560,336]{0,1:T(8,128)(2,1)} %param.7) | copy-start | bytes 5160964
  8.7 165.5 %all-to-all-start = ((bf16[8,5,336,256]{3,2,1,0:T(8,128)(2,1)}), bf16[8,5,336,256]{3,2,1,0:T(8,128)(2,1)}, u32[]{:S(2)}, u32[]{:S(2)}) async-start(bf16[8,5,336,256]{3,2,1,0:T(8,128)(2,1)} %shard_map.74), calls=%async_computation | async-start | bytes 13762560 | tf_op jit(solution)/shard_map/all_to_all | solution.py:115
  14.0 178.1 %collective-permute-start.1 = (bf16[4,40,64,256]{3,2,1,0:T(8,128)(2,1)}, bf16[4,40,64,256]{3,2,1,0:T(8,128)(2,1)}, u32[]{:S(2)}, u32[]{:S(2)}) collective-permute-start(bf16[4,40,64,256]{3,2,1,0:T(8,128)(2,1)} %param.9), channel_id=1, source_target_pairs={{0,1},{1,0},{2,3},{3,2},{4,5},{5,4},{6,7},{7,6},{8,9},{9,8},{10,11... | collective-permute-start | bytes 15728648 | tf_op jit(solution)/shard_map/ppermute | solution.py:59
  16.8 149.9 %collective-permute-start = (bf16[2560,336]{0,1:T(8,128)(2,1)S(1)}, bf16[2560,336]{0,1:T(8,128)(2,1)S(1)}, u32[]{:S(2)}, u32[]{:S(2)}) collective-permute-start(bf16[2560,336]{0,1:T(8,128)(2,1)S(1)} %copy-done.1), channel_id=1, source_target_pairs={{0,2},{1,3},{2,0},{3,1},{4,6},{5,7},{6,4},{7,5},{8,10},{9,11},{10,... | collective-permute-start | bytes 5160968 | tf_op jit(solution)/shard_map/ppermute | solution.py:53
  166.6 1.2 copy-start.2
  174.3 6.6 %copy-start.3 = (f32[1024]{0:T(1024)S(1)}, f32[1024]{0:T(1024)}, u32[]{:S(2)}) copy-start(f32[1024]{0:T(1024)} %param.11) | copy-start | bytes 12292
  174.3 6.6 %copy-start.4 = (f32[1024]{0:T(1024)S(1)}, f32[1024]{0:T(1024)}, u32[]{:S(2)}) copy-start(f32[1024]{0:T(1024)} %param.12) | copy-start | bytes 12292
  174.3 82.8 %all-to-all-start.1 = ((bf16[8,5,336,256]{3,2,1,0:T(8,128)(2,1)}), bf16[8,5,336,256]{3,2,1,0:T(8,128)(2,1)}, u32[]{:S(2)}, u32[]{:S(2)}) async-start(bf16[8,5,336,256]{3,2,1,0:T(8,128)(2,1)} %shard_map.73), calls=%async_computation.1 | async-start | bytes 13762560 | tf_op jit(solution)/shard_map/all_to_all | solution.py:115
  219.3 45.4 %slice-start = ((s8[5242880]{0:T(1024)(128)(4,1)}), s8[1048576]{0:T(1024)(128)(4,1)S(1)}, s32[]{:S(2)}) async-start(s8[5242880]{0:T(1024)(128)(4,1)} %bitcast.65), calls=%async_computation.3 | async-start | bytes 2097152
  257.1 7.6 %slice-start.1 = ((s8[5242880]{0:T(1024)(128)(4,1)}), s8[4194304]{0:T(1024)(128)(4,1)S(1)}, s32[]{:S(2)}) async-start(s8[5242880]{0:T(1024)(128)(4,1)} %bitcast.65), calls=%async_computation.4 | async-start | bytes 8388608
  287.9 7.1 %collective-permute-start.2 = (f32[64,336]{1,0:T(8,128)S(1)}, f32[64,336]{1,0:T(8,128)S(1)}, u32[]{:S(2)}, u32[]{:S(2)}) collective-permute-start(f32[64,336]{1,0:T(8,128)S(1)} %slice.13), channel_id=1, source_target_pairs={{0,2},{1,3},{2,0},{3,1},{4,6},{5,7},{6,4},{7,5},{8,10},{9,11},{10,... | collective-permute-start | bytes 258056 | tf_op jit(solution)/shard_map/ppermute | solution.py:146

commit v4 on v3

--- a/solution.py
+++ b/solution.py
@@ -137,14 +137,24 @@
             total = term if total is None else total + term
         totals.append(total.astype(jnp.bfloat16).reshape(sites, buses // sites, width))
 
-    stacked = jnp.concatenate(totals, axis=2)
-    shares = lax.all_to_all(stacked, "site", split_axis=0, concat_axis=0, tiled=True)
-    mine = jnp.sum(shares.astype(jnp.float32), axis=0)
-    result = mine[:, :width]
-    for s in range(1, halves):
-        back = [(z, (z - 2 * s) % groups) for z in range(groups)]
-        result = result + lax.ppermute(mine[:, s * width : (s + 1) * width], "scen", back)
-    return result
+    order = jnp.mod(group // 2 - jnp.arange(halves, dtype=jnp.int32), halves)
+    stacked = jnp.stack(totals, axis=1)[:, order] if halves > 2 else jnp.where(
+        group // 2 == 0, jnp.stack(totals, axis=1), jnp.stack(totals[::-1], axis=1)
+    )
+    stacked = stacked.reshape(sites * halves, buses // sites, width)
+    members = [
+        [k * groups + 2 * h + parity for k in range(sites) for h in range(halves)]
+        for parity in range(2)
+    ]
+    shares = lax.all_to_all(
+        stacked,
+        ("site", "scen"),
+        split_axis=0,
+        concat_axis=0,
+        axis_index_groups=members,
+        tiled=True,
+    )
+    return jnp.sum(shares.astype(jnp.float32), axis=0)
 
 
 def solution(mesh):

time: 296 us -> 300 us (1.014)
  blocking collectives: 14.9 us -> 26 us
  starting transfers between devices: 19 us -> 15.6 us
  waiting for transfers between devices: 188 us -> 185 us
    all_to_all x1, blocking collectives: 14.9 us -> 26 us  [shards(): lax.all_to_all(stacked, ('site', 'scen'), split_axis=0, concat_axis=0, ax...]
    ppermute x1 -> x0, waiting for transfers between devices: 3.65 us -> none  [shards(): lax.ppermute(mine[:, s * width:(s + 1) * width], 'scen', back)]
    ppermute x1 -> x0, starting transfers between devices: 3.45 us -> none  [shards(): lax.ppermute(mine[:, s * width:(s + 1) * width], 'scen', back)]
  transfers between devices with their start and end apart: 5 -> 4, of which waited for: 3 -> 2; matrix products, arithmetic and copies ran while one was open for 14% -> 14% of each run, Pallas kernels for 2% -> 2%
where the time goes in v4:
time: 300 us
  waiting for transfers between devices  185 us (62%)
  matrix products  29.9 us (10%)
  local copies, waits for them, and re-layouts  27.9 us (9%)
  blocking collectives  26 us (9%)
  starting transfers between devices  15.6 us (5%)
  Pallas kernels  12.9 us (4%)
    ppermute x1, waiting for transfers between devices, shards(): parts.append(lax.ppermute(normals, 'scen', moved))  147 us
    all_to_all x2, waiting for transfers between devices, shards(): lax.all_to_all(outgoing, 'site', split_axis=0, concat_axis=0, tiled=True)  37.3 us
    dot_general x4, matrix products, shards(): jnp.einsum('ksij,swj->kiw', portion, blocks, preferred_element_type=jnp.f...  27.4 us
    all_to_all x1, blocking collectives, shards(): lax.all_to_all(stacked, ('site', 'scen'), split_axis=0, concat_axis=0, ax...  26 us
    gather x2, local copies, waits for them, and re-layouts, in_slot_order(): ordered = flat[place[first:first + count] + rows * NZ]  20.5 us
    pallas_call x2, Pallas kernels, pick(): pl.pallas_call(pick_body, grid_spec=pltpu.PrefetchScalarGridSpec(num_scal...  12.9 us
    all_to_all x2, starting transfers between devices, shards(): lax.all_to_all(outgoing, 'site', split_axis=0, concat_axis=0, tiled=True)  10.3 us
  transfers between devices with their start and end apart: 4, of which 2 were waited for; matrix products, arithmetic and copies ran while one was open for 14% of the time, Pallas kernels for 2%

profile of v4, /device:TPU:0, one launch (start us, length us, event | category | flops | bytes accessed | tf_op | source)
XLA Modules:
  0.0 299.5 jit_solution(14595226069875370931)
XLA Ops:
  0.0 0.0 copy-start
  0.0 0.8 eq.57
  0.8 0.3 fusion.22
  1.1 0.1 broadcast_compare_fusion
  1.2 0.2 reduce_window_sum.18
  1.3 0.2 select_reduce_fusion.2
  1.5 0.7 copy.23.index_ref
  2.2 6.5 %shard_map.74 = bf16[8,5,336,256]{3,2,1,0:T(8,128)(2,1)} custom-call(s32[8,5]{1,0:T(8,128)} %copy.23.index_ref, bf16[336,2560]{1,0:T(8,128)(2,1)} %bitcast.72), custom_call_target="tpu_custom_call" | custom-call | bytes 13762560 | tf_op jit(solution)/shard_map/pallas_call | solution.py:25
  8.7 5.3 %all-to-all-start = ((bf16[8,5,336,256]{3,2,1,0:T(8,128)(2,1)}), bf16[8,5,336,256]{3,2,1,0:T(8,128)(2,1)}, u32[]{:S(2)}, u32[]{:S(2)}) async-start(bf16[8,5,336,256]{3,2,1,0:T(8,128)(2,1)} %shard_map.74), calls=%async_computation | async-start | bytes 13762560 | tf_op jit(solution)/shard_map/all_to_all | solution.py:115
  14.0 2.7 collective-permute-start.1
  16.8 2.6 collective-permute-start
  19.4 147.3 %collective-permute-done = bf16[2560,336]{0,1:T(8,128)(2,1)S(1)} collective-permute-done((bf16[2560,336]{0,1:T(8,128)(2,1)S(1)}, bf16[2560,336]{0,1:T(8,128)(2,1)S(1)}, u32[]{:S(2)}, u32[]{:S(2)}) %collective-permute-start) | collective-permute-done | bytes 1720352 | tf_op jit(solution)/shard_map/ppermute | solution.py:53
  166.6 1.2 copy-done.2
  167.8 6.4 %shard_map.73 = bf16[8,5,336,256]{3,2,1,0:T(8,128)(2,1)} custom-call(s32[8,5]{1,0:T(8,128)} %copy.23.index_ref, bf16[336,2560]{1,0:T(8,128)(2,1)} %bitcast.73), custom_call_target="tpu_custom_call" | custom-call | bytes 13762560 | tf_op jit(solution)/shard_map/pallas_call | solution.py:25
  174.3 0.0 all-to-all-done
  174.3 4.9 %all-to-all-start.1 = ((bf16[8,5,336,256]{3,2,1,0:T(8,128)(2,1)}), bf16[8,5,336,256]{3,2,1,0:T(8,128)(2,1)}, u32[]{:S(2)}, u32[]{:S(2)}) async-start(bf16[8,5,336,256]{3,2,1,0:T(8,128)(2,1)} %shard_map.73), calls=%async_computation.1 | async-start | bytes 13762560 | tf_op jit(solution)/shard_map/all_to_all | solution.py:115
  179.2 0.1 reshape.159
  179.3 0.2 reduce_window_sum.17
  179.5 0.1 sub.49
  179.6 0.7 constant_dynamic-slice_fusion.4
  180.3 0.2 select_reduce_fusion.1
  180.5 0.2 select_reduce_fusion
  180.7 0.1 compare_select_fusion
  180.7 0.1 reshape.162
  180.9 0.7 dynamic_slice.31
  181.6 0.1 constant_dynamic-slice_fusion
  181.6 0.1 eq.50
  181.7 0.1 eq.128
  181.8 10.3 %gather_fusion = bf16[160,64,256]{2,1,0:T(8,128)(2,1)} fusion(bf16[160,64,256]{2,1,0:T(8,128)(2,1)} %bitcast.64, s32[1024]{0:T(1024)S(1)} %pad_clamp_fusion), kind=kCustom, calls=%fused_computation | custom fusion | bytes 10486400 | tf_op jit(solution)/shard_map/gather | solution.py:90
  192.1 0.1 multiply_multiply_fusion
  192.2 0.0 collective-permute-done.1
  192.2 10.2 %gather_fusion.1 = bf16[160,64,256]{2,1,0:T(8,128)(2,1)} fusion(bf16[160,64,256]{2,1,0:T(8,128)(2,1)} %bitcast.11, s32[1024]{0:T(1024)S(1)} %pad_clamp_fusion), kind=kCustom, calls=%fused_computation.1 | custom fusion | bytes 10486400 | tf_op jit(solution)/shard_map/gather | solution.py:90
  202.4 7.4 %fusion.19 = bf16[4,64,336]{2,1,0:T(8,128)(2,1)S(1)} fusion(bf16[4,40,64,256]{3,2,1,0:T(8,128)(2,1)} %bitcast.69, bf16[40,336,256,1]{2,1,0,3:T(8,128)(2,1)} %bitcast.6), kind=kOutput, calls=%fused_computation.32 | convolution fusion | flops 1761693696 | bytes 12296192 | tf_op jit(solution)/shard_map/ksij,swj->kiw/dot_general | solution.py:123
  209.8 0.1 reshape.152
  209.9 0.3 fusion.15
  210.2 0.3 copy.28
  210.5 0.2 reshape.153
  210.7 7.4 %fusion.18 = bf16[4,64,336]{2,1,0:T(8,128)(2,1)S(1)} fusion(bf16[4,40,64,256]{3,2,1,0:T(8,128)(2,1)} %bitcast.65, bf16[40,336,256,1]{2,1,0,3:T(8,128)(2,1)} %bitcast.6), kind=kOutput, calls=%fused_computation.31 | convolution fusion | flops 1761693696 | bytes 12296192 | tf_op jit(solution)/shard_map/ksij,swj->kiw/dot_general | solution.py:123
  218.1 0.1 reshape.149
  218.2 0.3 fusion.14
  218.5 0.3 copy.26
  218.8 0.2 reshape.150
  218.9 0.3 fusion.24
  219.3 0.0 slice-start
  219.3 0.3 fusion.12
  219.6 0.2 copy.29
  219.8 37.3 %all-to-all-done.1 = bf16[8,5,336,256]{3,2,1,0:T(8,128)(2,1)} async-done(((bf16[8,5,336,256]{3,2,1,0:T(8,128)(2,1)}), bf16[8,5,336,256]{3,2,1,0:T(8,128)(2,1)}, u32[]{:S(2)}, u32[]{:S(2)}) %all-to-all-start.1) | async-done | bytes 6881312 | tf_op jit(solution)/shard_map/all_to_all | solution.py:115
  257.1 7.5 %fusion.21 = bf16[4,64,336]{2,1,0:T(8,128)(2,1)S(1)} fusion(bf16[4,40,64,256]{3,2,1,0:T(8,128)(2,1)} %bitcast.70, bf16[40,336,256,1]{2,1,0,3:T(8,128)(2,1)} %bitcast.19), kind=kOutput, calls=%fused_computation.34 | convolution fusion | flops 1761693696 | bytes 12296192 | tf_op jit(solution)/shard_map/ksij,swj->kiw/dot_general | solution.py:123
  264.7 5.1 %fusion.20 = bf16[4,64,336]{2,1,0:T(8,128)(2,1)S(1)} fusion(bf16[4,40,64,256]{3,2,1,0:T(8,128)(2,1)S(1)} %bitcast.68, bf16[40,336,256,1]{2,1,0,3:T(8,128)(2,1)} %bitcast.19), kind=kOutput, calls=%fused_computation.33 | convolution fusion | flops 1761693696 | bytes 12296192 | tf_op jit(solution)/shard_map/ksij,swj->kiw/dot_general | solution.py:123
  269.8 0.1 reshape.157
  269.9 0.3 fusion.17
  270.2 0.3 copy.33
  270.5 0.2 reshape.158
  270.7 0.1 reshape.155
  270.8 0.3 fusion.16
  271.1 0.3 copy.31
  271.4 0.2 reshape.156
  271.5 0.3 fusion.23
  271.9 0.3 fusion.13
  272.2 0.2 copy.34
  272.4 0.2 maximum_select_fusion
  272.7 0.1 copy.35
  272.8 26.0 %all_to_all.15 = bf16[16,64,336]{2,1,0:T(8,128)(2,1)S(1)} all-to-all(bf16[16,64,336]{2,1,0:T(8,128)(2,1)S(1)} %bitcast.71), channel_id=1, replica_groups={{0,2,4,6,8,10,12,14,16,18,20,22,24,26,28,30},{1,3,5,7,9,11,13,15,17,19,..., dimensions={0} | all-to-all | bytes 1376256 | tf_op jit(solution)/shard_map/all_to_all | solution.py:149
  298.8 0.8 convert_reduce_fusion
  (21 shorter events, 0.1 us)
Async XLA Ops:
  0.0 209.9 %copy-start = (bf16[168,168]{1,0:T(8,128)(2,1)S(1)}, bf16[168,168]{1,0:T(8,128)(2,1)}, u32[]{:S(2)}) copy-start(bf16[168,168]{1,0:T(8,128)(2,1)} %param.10) | copy-start | bytes 169348
  8.7 8.1 %copy-start.1 = (bf16[2560,336]{0,1:T(8,128)(2,1)S(1)}, bf16[2560,336]{0,1:T(8,128)(2,1)}, u32[]{:S(2)}) copy-start(bf16[2560,336]{0,1:T(8,128)(2,1)} %param.7) | copy-start | bytes 5160964
  8.7 165.5 %all-to-all-start = ((bf16[8,5,336,256]{3,2,1,0:T(8,128)(2,1)}), bf16[8,5,336,256]{3,2,1,0:T(8,128)(2,1)}, u32[]{:S(2)}, u32[]{:S(2)}) async-start(bf16[8,5,336,256]{3,2,1,0:T(8,128)(2,1)} %shard_map.74), calls=%async_computation | async-start | bytes 13762560 | tf_op jit(solution)/shard_map/all_to_all | solution.py:115
  14.0 178.1 %collective-permute-start.1 = (bf16[4,40,64,256]{3,2,1,0:T(8,128)(2,1)}, bf16[4,40,64,256]{3,2,1,0:T(8,128)(2,1)}, u32[]{:S(2)}, u32[]{:S(2)}) collective-permute-start(bf16[4,40,64,256]{3,2,1,0:T(8,128)(2,1)} %param.9), channel_id=1, source_target_pairs={{0,1},{1,0},{2,3},{3,2},{4,5},{5,4},{6,7},{7,6},{8,9},{9,8},{10,11... | collective-permute-start | bytes 15728648 | tf_op jit(solution)/shard_map/ppermute | solution.py:59
  16.8 149.9 %collective-permute-start = (bf16[2560,336]{0,1:T(8,128)(2,1)S(1)}, bf16[2560,336]{0,1:T(8,128)(2,1)S(1)}, u32[]{:S(2)}, u32[]{:S(2)}) collective-permute-start(bf16[2560,336]{0,1:T(8,128)(2,1)S(1)} %copy-done.1), channel_id=1, source_target_pairs={{0,2},{1,3},{2,0},{3,1},{4,6},{5,7},{6,4},{7,5},{8,10},{9,11},{10,... | collective-permute-start | bytes 5160968 | tf_op jit(solution)/shard_map/ppermute | solution.py:53
  166.6 1.2 copy-start.2
  174.3 6.6 %copy-start.3 = (f32[1024]{0:T(1024)S(1)}, f32[1024]{0:T(1024)}, u32[]{:S(2)}) copy-start(f32[1024]{0:T(1024)} %param.11) | copy-start | bytes 12292
  174.3 6.6 %copy-start.4 = (f32[1024]{0:T(1024)S(1)}, f32[1024]{0:T(1024)}, u32[]{:S(2)}) copy-start(f32[1024]{0:T(1024)} %param.12) | copy-start | bytes 12292
  174.3 82.8 %all-to-all-start.1 = ((bf16[8,5,336,256]{3,2,1,0:T(8,128)(2,1)}), bf16[8,5,336,256]{3,2,1,0:T(8,128)(2,1)}, u32[]{:S(2)}, u32[]{:S(2)}) async-start(bf16[8,5,336,256]{3,2,1,0:T(8,128)(2,1)} %shard_map.73), calls=%async_computation.1 | async-start | bytes 13762560 | tf_op jit(solution)/shard_map/all_to_all | solution.py:115
  219.3 45.4 %slice-start = ((s8[5242880]{0:T(1024)(128)(4,1)}), s8[1048576]{0:T(1024)(128)(4,1)S(1)}, s32[]{:S(2)}) async-start(s8[5242880]{0:T(1024)(128)(4,1)} %bitcast.66), calls=%async_computation.3 | async-start | bytes 2097152
  257.1 7.6 %slice-start.1 = ((s8[5242880]{0:T(1024)(128)(4,1)}), s8[4194304]{0:T(1024)(128)(4,1)S(1)}, s32[]{:S(2)}) async-start(s8[5242880]{0:T(1024)(128)(4,1)} %bitcast.66), calls=%async_computation.4 | async-start | bytes 8388608

commit v5 on v3

--- a/solution.py
+++ b/solution.py
@@ -1,3 +1,5 @@
+import functools
+
 import jax
 import jax.numpy as jnp
 from jax import lax
@@ -35,6 +37,61 @@
             flops=0, bytes_accessed=2 * sites * slots * width * BLK * 2, transcendentals=0
         ),
     )(index, table)
+
+
+def exchange_body(sites, groups, *refs):
+    halves = groups // 2
+    share_refs = refs[:halves]
+    out_ref, landed, send_sem, recv_sem = refs[halves:]
+    own = lax.axis_index("site")
+    group = lax.axis_index("scen")
+    offsets = [(a, h) for a in range(sites) for h in range(halves)][1:]
+    peers = [
+        (lax.rem(own + a, sites), lax.rem(group + 2 * h, groups)) for a, h in offsets
+    ]
+    barrier = pltpu.get_barrier_semaphore()
+    for peer in peers:
+        pl.semaphore_signal(
+            barrier, inc=1, device_id=peer, device_id_type=pl.DeviceIdType.MESH
+        )
+    pl.semaphore_wait(barrier, len(peers))
+    copies = []
+    for n, ((_, h), peer) in enumerate(zip(offsets, peers)):
+        copies.append(
+            pltpu.make_async_remote_copy(
+                src_ref=share_refs[(halves - h) % halves].at[peer[0]],
+                dst_ref=landed.at[n],
+                send_sem=send_sem.at[n],
+                recv_sem=recv_sem.at[n],
+                device_id=peer,
+                device_id_type=pl.DeviceIdType.MESH,
+            )
+        )
+        copies[-1].start()
+    total = share_refs[0][own].astype(jnp.float32)
+    for n, copy in enumerate(copies):
+        copy.wait_recv()
+        total = total + landed[n].astype(jnp.float32)
+    for copy in copies:
+        copy.wait_send()
+    out_ref[...] = total
+
+
+def exchange(shares, sites, groups):
+    _, height, width = shares[0].shape
+    count = sites * len(shares) - 1
+    return pl.pallas_call(
+        functools.partial(exchange_body, sites, groups),
+        out_shape=jax.ShapeDtypeStruct((height, width), jnp.float32),
+        in_specs=[pl.BlockSpec(memory_space=pltpu.VMEM)] * len(shares),
+        out_specs=pl.BlockSpec(memory_space=pltpu.VMEM),
+        scratch_shapes=[
+            pltpu.VMEM((count, height, width), shares[0].dtype),
+            pltpu.SemaphoreType.DMA((count,)),
+            pltpu.SemaphoreType.DMA((count,)),
+        ],
+        compiler_params=pltpu.CompilerParams(collective_id=0, has_side_effects=True),
+    )(*shares)
 
 
 def shards(normals, pattern, factor, temporal, capacity, spread, bus_map, buses):
@@ -137,14 +194,7 @@
             total = term if total is None else total + term
         totals.append(total.astype(jnp.bfloat16).reshape(sites, buses // sites, width))
 
-    stacked = jnp.concatenate(totals, axis=2)
-    shares = lax.all_to_all(stacked, "site", split_axis=0, concat_axis=0, tiled=True)
-    mine = jnp.sum(shares.astype(jnp.float32), axis=0)
-    result = mine[:, :width]
-    for s in range(1, halves):
-        back = [(z, (z - 2 * s) % groups) for z in range(groups)]
-        result = result + lax.ppermute(mine[:, s * width : (s + 1) * width], "scen", back)
-    return result
+    return exchange(totals, sites, groups)
 
 
 def solution(mesh):

time: 296 us -> 300 us (1.014)
  Pallas kernels: 12.9 us -> 37.1 us
  blocking collectives: 14.9 us -> 0 us
  waiting for transfers between devices: 188 us -> 184 us
  starting transfers between devices: 19 us -> 15.6 us
    pallas_call x0 -> x1, Pallas kernels: none -> 24.2 us  [exchange(): pl.pallas_call(functools.partial(exchange_body, sites, groups), out_shape...]
    all_to_all x1 -> x0, blocking collectives: 14.9 us -> none  [shards(): lax.all_to_all(stacked, 'site', split_axis=0, concat_axis=0, tiled=True)]
    ppermute x1 -> x0, waiting for transfers between devices: 3.65 us -> none  [shards(): lax.ppermute(mine[:, s * width:(s + 1) * width], 'scen', back)]
    ppermute x1 -> x0, starting transfers between devices: 3.45 us -> none  [shards(): lax.ppermute(mine[:, s * width:(s + 1) * width], 'scen', back)]
  transfers between devices with their start and end apart: 5 -> 4, of which waited for: 3 -> 2; matrix products, arithmetic and copies ran while one was open for 14% -> 14% of each run, Pallas kernels for 2% -> 2%
where the time goes in v5:
time: 300 us; the launch traced here: 299 us
  waiting for transfers between devices  184 us (61%)
  Pallas kernels  37.1 us (12%)
  local copies, waits for them, and re-layouts  30.7 us (10%)
  matrix products  29.9 us (10%)
  starting transfers between devices  15.6 us (5%)
    ppermute x1, waiting for transfers between devices, shards(): parts.append(lax.ppermute(normals, 'scen', moved))  147 us
    all_to_all x2, waiting for transfers between devices, shards(): lax.all_to_all(outgoing, 'site', split_axis=0, concat_axis=0, tiled=True)  36.6 us
    dot_general x4, matrix products, shards(): jnp.einsum('ksij,swj->kiw', portion, blocks, preferred_element_type=jnp.f...  27.4 us
    pallas_call x1, Pallas kernels, exchange(): pl.pallas_call(functools.partial(exchange_body, sites, groups), out_shape...  24.2 us
    gather x2, local copies, waits for them, and re-layouts, in_slot_order(): ordered = flat[place[first:first + count] + rows * NZ]  20.5 us
    pallas_call x2, Pallas kernels, pick(): pl.pallas_call(pick_body, grid_spec=pltpu.PrefetchScalarGridSpec(num_scal...  12.9 us
    all_to_all x2, starting transfers between devices, shards(): lax.all_to_all(outgoing, 'site', split_axis=0, concat_axis=0, tiled=True)  10.3 us
  transfers between devices with their start and end apart: 4, of which 2 were waited for; matrix products, arithmetic and copies ran while one was open for 14% of the time, Pallas kernels for 2%

profile of v5, /device:TPU:0, one launch (start us, length us, event | category | flops | bytes accessed | tf_op | source)
XLA Modules:
  0.0 298.9 jit_solution(10585939703766166031)
XLA Ops:
  0.0 0.0 copy-start
  0.0 0.8 eq.54
  0.8 0.3 fusion.22
  1.1 0.1 broadcast_compare_fusion
  1.2 0.2 reduce_window_sum.18
  1.3 0.2 select_reduce_fusion.2
  1.5 0.7 copy.24.index_ref
  2.2 6.5 %shard_map.74 = bf16[8,5,336,256]{3,2,1,0:T(8,128)(2,1)} custom-call(s32[8,5]{1,0:T(8,128)} %copy.24.index_ref, bf16[336,2560]{1,0:T(8,128)(2,1)} %bitcast.70), custom_call_target="tpu_custom_call" | custom-call | bytes 13762560 | tf_op jit(solution)/shard_map/pallas_call | solution.py:27
  8.7 5.3 %all-to-all-start = ((bf16[8,5,336,256]{3,2,1,0:T(8,128)(2,1)}), bf16[8,5,336,256]{3,2,1,0:T(8,128)(2,1)}, u32[]{:S(2)}, u32[]{:S(2)}) async-start(bf16[8,5,336,256]{3,2,1,0:T(8,128)(2,1)} %shard_map.74), calls=%async_computation | async-start | bytes 13762560 | tf_op jit(solution)/shard_map/all_to_all | solution.py:172
  14.0 2.7 collective-permute-start.1
  16.8 2.6 collective-permute-start
  19.4 147.3 %collective-permute-done = bf16[2560,336]{0,1:T(8,128)(2,1)S(1)} collective-permute-done((bf16[2560,336]{0,1:T(8,128)(2,1)S(1)}, bf16[2560,336]{0,1:T(8,128)(2,1)S(1)}, u32[]{:S(2)}, u32[]{:S(2)}) %collective-permute-start) | collective-permute-done | bytes 1720352 | tf_op jit(solution)/shard_map/ppermute | solution.py:110
  166.6 1.2 copy-done.2
  167.8 6.4 %shard_map.73 = bf16[8,5,336,256]{3,2,1,0:T(8,128)(2,1)} custom-call(s32[8,5]{1,0:T(8,128)} %copy.24.index_ref, bf16[336,2560]{1,0:T(8,128)(2,1)} %bitcast.71), custom_call_target="tpu_custom_call" | custom-call | bytes 13762560 | tf_op jit(solution)/shard_map/pallas_call | solution.py:27
  174.3 0.0 all-to-all-done
  174.3 4.9 %all-to-all-start.1 = ((bf16[8,5,336,256]{3,2,1,0:T(8,128)(2,1)}), bf16[8,5,336,256]{3,2,1,0:T(8,128)(2,1)}, u32[]{:S(2)}, u32[]{:S(2)}) async-start(bf16[8,5,336,256]{3,2,1,0:T(8,128)(2,1)} %shard_map.73), calls=%async_computation.1 | async-start | bytes 13762560 | tf_op jit(solution)/shard_map/all_to_all | solution.py:172
  179.2 0.1 reshape.162
  179.3 0.2 reduce_window_sum.17
  179.5 0.1 sub.44
  179.6 0.7 constant_dynamic-slice_fusion.4
  180.3 0.2 select_reduce_fusion.1
  180.5 0.2 select_reduce_fusion
  180.7 0.1 compare_select_fusion
  180.7 0.1 reshape.165
  180.8 0.0 copy-done.3
  180.8 0.0 copy-done.4
  180.9 0.7 dynamic_slice.31
  181.6 0.1 constant_dynamic-slice_fusion
  181.6 0.1 eq.47
  181.7 0.1 eq.124
  181.8 10.3 %gather_fusion = bf16[160,64,256]{2,1,0:T(8,128)(2,1)} fusion(bf16[160,64,256]{2,1,0:T(8,128)(2,1)} %bitcast.63, s32[1024]{0:T(1024)S(1)} %pad_clamp_fusion), kind=kCustom, calls=%fused_computation | custom fusion | bytes 10486400 | tf_op jit(solution)/shard_map/gather | solution.py:147
  192.1 0.1 multiply_multiply_fusion
  192.1 0.0 collective-permute-done.1
  192.2 10.2 %gather_fusion.1 = bf16[160,64,256]{2,1,0:T(8,128)(2,1)} fusion(bf16[160,64,256]{2,1,0:T(8,128)(2,1)} %bitcast.11, s32[1024]{0:T(1024)S(1)} %pad_clamp_fusion), kind=kCustom, calls=%fused_computation.1 | custom fusion | bytes 10486400 | tf_op jit(solution)/shard_map/gather | solution.py:147
  202.4 7.4 %fusion.19 = bf16[4,64,336]{2,1,0:T(8,128)(2,1)S(1)} fusion(bf16[4,40,64,256]{3,2,1,0:T(8,128)(2,1)} %bitcast.68, bf16[40,336,256,1]{2,1,0,3:T(8,128)(2,1)} %bitcast.6), kind=kOutput, calls=%fused_computation.31 | convolution fusion | flops 1761693696 | bytes 12296192 | tf_op jit(solution)/shard_map/ksij,swj->kiw/dot_general | solution.py:180
  209.8 0.1 reshape.153
  209.9 0.3 fusion.15
  210.2 0.3 copy.29
  210.5 0.2 reshape.154
  210.7 7.4 %fusion.18 = bf16[4,64,336]{2,1,0:T(8,128)(2,1)S(1)} fusion(bf16[4,40,64,256]{3,2,1,0:T(8,128)(2,1)} %bitcast.64, bf16[40,336,256,1]{2,1,0,3:T(8,128)(2,1)} %bitcast.6), kind=kOutput, calls=%fused_computation.30 | convolution fusion | flops 1761693696 | bytes 12296192 | tf_op jit(solution)/shard_map/ksij,swj->kiw/dot_general | solution.py:180
  218.1 0.1 reshape.150
  218.2 0.3 fusion.14
  218.5 0.3 copy.27
  218.8 0.2 reshape.151
  218.9 0.3 fusion.24
  219.3 0.0 slice-start
  219.3 0.3 fusion.12
  219.6 0.9 copy.30
  220.5 36.6 %all-to-all-done.1 = bf16[8,5,336,256]{3,2,1,0:T(8,128)(2,1)} async-done(((bf16[8,5,336,256]{3,2,1,0:T(8,128)(2,1)}), bf16[8,5,336,256]{3,2,1,0:T(8,128)(2,1)}, u32[]{:S(2)}, u32[]{:S(2)}) %all-to-all-start.1) | async-done | bytes 6881312 | tf_op jit(solution)/shard_map/all_to_all | solution.py:172
  257.1 7.5 %fusion.21 = bf16[4,64,336]{2,1,0:T(8,128)(2,1)S(1)} fusion(bf16[4,40,64,256]{3,2,1,0:T(8,128)(2,1)} %bitcast.69, bf16[40,336,256,1]{2,1,0,3:T(8,128)(2,1)} %bitcast.19), kind=kOutput, calls=%fused_computation.33 | convolution fusion | flops 1761693696 | bytes 12296192 | tf_op jit(solution)/shard_map/ksij,swj->kiw/dot_general | solution.py:180
  264.7 5.1 %fusion.20 = bf16[4,64,336]{2,1,0:T(8,128)(2,1)S(1)} fusion(bf16[4,40,64,256]{3,2,1,0:T(8,128)(2,1)S(1)} %bitcast.67, bf16[40,336,256,1]{2,1,0,3:T(8,128)(2,1)} %bitcast.19), kind=kOutput, calls=%fused_computation.32 | convolution fusion | flops 1761693696 | bytes 12296192 | tf_op jit(solution)/shard_map/ksij,swj->kiw/dot_general | solution.py:180
  269.8 0.1 reshape.159
  269.9 0.3 fusion.17
  270.2 0.3 copy.34
  270.5 0.2 reshape.160
  270.7 0.1 reshape.157
  270.8 0.3 fusion.16
  271.1 0.3 copy.32
  271.4 0.2 reshape.158
  271.5 0.3 fusion.23
  271.9 0.3 fusion.13
  272.2 0.9 copy.35
  273.1 24.2 %shard_map.75 = f32[64,336]{1,0:T(8,128)} custom-call(bf16[8,64,336]{2,1,0:T(8,128)(2,1)} %bitcast.72, bf16[8,64,336]{2,1,0:T(8,128)(2,1)} %bitcast.73), custom_call_target="tpu_custom_call" | custom-call | tf_op jit(solution)/shard_map/pallas_call | solution.py:83
  297.3 1.5 copy.50
  (19 shorter events, 0.1 us)
Async XLA Ops:
  0.0 209.9 %copy-start = (bf16[168,168]{1,0:T(8,128)(2,1)S(1)}, bf16[168,168]{1,0:T(8,128)(2,1)}, u32[]{:S(2)}) copy-start(bf16[168,168]{1,0:T(8,128)(2,1)} %param.10) | copy-start | bytes 169348
  8.7 8.1 %copy-start.1 = (bf16[2560,336]{0,1:T(8,128)(2,1)S(1)}, bf16[2560,336]{0,1:T(8,128)(2,1)}, u32[]{:S(2)}) copy-start(bf16[2560,336]{0,1:T(8,128)(2,1)} %param.7) | copy-start | bytes 5160964
  8.7 165.5 %all-to-all-start = ((bf16[8,5,336,256]{3,2,1,0:T(8,128)(2,1)}), bf16[8,5,336,256]{3,2,1,0:T(8,128)(2,1)}, u32[]{:S(2)}, u32[]{:S(2)}) async-start(bf16[8,5,336,256]{3,2,1,0:T(8,128)(2,1)} %shard_map.74), calls=%async_computation | async-start | bytes 13762560 | tf_op jit(solution)/shard_map/all_to_all | solution.py:172
  14.0 178.1 %collective-permute-start.1 = (bf16[4,40,64,256]{3,2,1,0:T(8,128)(2,1)}, bf16[4,40,64,256]{3,2,1,0:T(8,128)(2,1)}, u32[]{:S(2)}, u32[]{:S(2)}) collective-permute-start(bf16[4,40,64,256]{3,2,1,0:T(8,128)(2,1)} %param.9), channel_id=1, source_target_pairs={{0,1},{1,0},{2,3},{3,2},{4,5},{5,4},{6,7},{7,6},{8,9},{9,8},{10,11... | collective-permute-start | bytes 15728648 | tf_op jit(solution)/shard_map/ppermute | solution.py:116
  16.8 149.9 %collective-permute-start = (bf16[2560,336]{0,1:T(8,128)(2,1)S(1)}, bf16[2560,336]{0,1:T(8,128)(2,1)S(1)}, u32[]{:S(2)}, u32[]{:S(2)}) collective-permute-start(bf16[2560,336]{0,1:T(8,128)(2,1)S(1)} %copy-done.1), channel_id=1, source_target_pairs={{0,2},{1,3},{2,0},{3,1},{4,6},{5,7},{6,4},{7,5},{8,10},{9,11},{10,... | collective-permute-start | bytes 5160968 | tf_op jit(solution)/shard_map/ppermute | solution.py:110
  166.6 1.2 copy-start.2
  174.3 6.6 %copy-start.3 = (f32[1024]{0:T(1024)S(1)}, f32[1024]{0:T(1024)}, u32[]{:S(2)}) copy-start(f32[1024]{0:T(1024)} %param.11) | copy-start | bytes 12292
  174.3 6.6 %copy-start.4 = (f32[1024]{0:T(1024)S(1)}, f32[1024]{0:T(1024)}, u32[]{:S(2)}) copy-start(f32[1024]{0:T(1024)} %param.12) | copy-start | bytes 12292
  174.3 82.8 %all-to-all-start.1 = ((bf16[8,5,336,256]{3,2,1,0:T(8,128)(2,1)}), bf16[8,5,336,256]{3,2,1,0:T(8,128)(2,1)}, u32[]{:S(2)}, u32[]{:S(2)}) async-start(bf16[8,5,336,256]{3,2,1,0:T(8,128)(2,1)} %shard_map.73), calls=%async_computation.1 | async-start | bytes 13762560 | tf_op jit(solution)/shard_map/all_to_all | solution.py:172
  219.3 45.4 %slice-start = ((s8[5242880]{0:T(1024)(128)(4,1)}), s8[1048576]{0:T(1024)(128)(4,1)S(1)}, s32[]{:S(2)}) async-start(s8[5242880]{0:T(1024)(128)(4,1)} %bitcast.65), calls=%async_computation.2 | async-start | bytes 2097152
  257.1 7.6 %slice-start.1 = ((s8[5242880]{0:T(1024)(128)(4,1)}), s8[4194304]{0:T(1024)(128)(4,1)S(1)}, s32[]{:S(2)}) async-start(s8[5242880]{0:T(1024)(128)(4,1)} %bitcast.65), calls=%async_computation.3 | async-start | bytes 8388608

commit v6 on v5

--- a/solution.py
+++ b/solution.py
@@ -45,10 +45,7 @@
     out_ref, landed, send_sem, recv_sem = refs[halves:]
     own = lax.axis_index("site")
     group = lax.axis_index("scen")
-    offsets = [(a, h) for a in range(sites) for h in range(halves)][1:]
-    peers = [
-        (lax.rem(own + a, sites), lax.rem(group + 2 * h, groups)) for a, h in offsets
-    ]
+    peers = [(lax.rem(own + a, sites), group) for a in range(1, sites)]
     barrier = pltpu.get_barrier_semaphore()
     for peer in peers:
         pl.semaphore_signal(
@@ -56,39 +53,41 @@
         )
     pl.semaphore_wait(barrier, len(peers))
     copies = []
-    for n, ((_, h), peer) in enumerate(zip(offsets, peers)):
-        copies.append(
-            pltpu.make_async_remote_copy(
-                src_ref=share_refs[(halves - h) % halves].at[peer[0]],
-                dst_ref=landed.at[n],
-                send_sem=send_sem.at[n],
-                recv_sem=recv_sem.at[n],
-                device_id=peer,
-                device_id_type=pl.DeviceIdType.MESH,
+    for h in range(halves):
+        for n, peer in enumerate(peers):
+            copies.append(
+                pltpu.make_async_remote_copy(
+                    src_ref=share_refs[h].at[peer[0]],
+                    dst_ref=landed.at[h, n],
+                    send_sem=send_sem.at[h, n],
+                    recv_sem=recv_sem.at[h, n],
+                    device_id=peer,
+                    device_id_type=pl.DeviceIdType.MESH,
+                )
             )
-        )
-        copies[-1].start()
-    total = share_refs[0][own].astype(jnp.float32)
-    for n, copy in enumerate(copies):
-        copy.wait_recv()
-        total = total + landed[n].astype(jnp.float32)
+            copies[-1].start()
+    for h in range(halves):
+        total = share_refs[h][own].astype(jnp.float32)
+        for n in range(len(peers)):
+            copies[h * len(peers) + n].wait_recv()
+            total = total + landed[h, n].astype(jnp.float32)
+        out_ref[h] = total
     for copy in copies:
         copy.wait_send()
-    out_ref[...] = total
 
 
 def exchange(shares, sites, groups):
     _, height, width = shares[0].shape
-    count = sites * len(shares) - 1
+    slots = (len(shares), sites - 1)
     return pl.pallas_call(
         functools.partial(exchange_body, sites, groups),
-        out_shape=jax.ShapeDtypeStruct((height, width), jnp.float32),
+        out_shape=jax.ShapeDtypeStruct((len(shares), height, width), jnp.float32),
         in_specs=[pl.BlockSpec(memory_space=pltpu.VMEM)] * len(shares),
         out_specs=pl.BlockSpec(memory_space=pltpu.VMEM),
         scratch_shapes=[
-            pltpu.VMEM((count, height, width), shares[0].dtype),
-            pltpu.SemaphoreType.DMA((count,)),
-            pltpu.SemaphoreType.DMA((count,)),
+            pltpu.VMEM((*slots, height, width), shares[0].dtype),
+            pltpu.SemaphoreType.DMA(slots),
+            pltpu.SemaphoreType.DMA(slots),
         ],
         compiler_params=pltpu.CompilerParams(collective_id=0, has_side_effects=True),
     )(*shares)
@@ -194,7 +193,12 @@
             total = term if total is None else total + term
         totals.append(total.astype(jnp.bfloat16).reshape(sites, buses // sites, width))
 
-    return exchange(totals, sites, groups)
+    mine = exchange(totals, sites, groups)
+    result = mine[0]
+    for s in range(1, halves):
+        back = [(z, (z - 2 * s) % groups) for z in range(groups)]
+        result = result + lax.ppermute(mine[s], "scen", back)
+    return result
 
 
 def solution(mesh):

time: 300 us -> 296 us (0.987)
  Pallas kernels: 37.1 us -> 26 us
  starting transfers between devices: 15.6 us -> 19 us
  waiting for transfers between devices: 184 us -> 187 us
    pallas_call x1, Pallas kernels: 24.2 us -> 13 us  [exchange(): pl.pallas_call(functools.partial(exchange_body, sites, groups), out_shape...]
    ppermute x0 -> x1, starting transfers between devices: none -> 3.38 us  [shards(): result = result + lax.ppermute(mine[s], 'scen', back)]
    ppermute x0 -> x1, waiting for transfers between devices: none -> 3.3 us  [shards(): result = result + lax.ppermute(mine[s], 'scen', back)]
  transfers between devices with their start and end apart: 4 -> 5, of which waited for: 2 -> 3; matrix products, arithmetic and copies ran while one was open for 14% -> 14% of each run, Pallas kernels for 2% -> 2%
where the time goes in v6:
time: 296 us; the launch traced here: 295 us
  waiting for transfers between devices  187 us (63%)
  local copies, waits for them, and re-layouts  30.1 us (10%)
  matrix products  29.9 us (10%)
  Pallas kernels  26 us (9%)
  starting transfers between devices  19 us (6%)
    ppermute x1, waiting for transfers between devices, shards(): parts.append(lax.ppermute(normals, 'scen', moved))  147 us
    all_to_all x2, waiting for transfers between devices, shards(): lax.all_to_all(outgoing, 'site', split_axis=0, concat_axis=0, tiled=True)  36.6 us
    dot_general x4, matrix products, shards(): jnp.einsum('ksij,swj->kiw', portion, blocks, preferred_element_type=jnp.f...  27.4 us
    gather x2, local copies, waits for them, and re-layouts, in_slot_order(): ordered = flat[place[first:first + count] + rows * NZ]  20.5 us
    pallas_call x1, Pallas kernels, exchange(): pl.pallas_call(functools.partial(exchange_body, sites, groups), out_shape...  13 us
    pallas_call x2, Pallas kernels, pick(): pl.pallas_call(pick_body, grid_spec=pltpu.PrefetchScalarGridSpec(num_scal...  12.9 us
    all_to_all x2, starting transfers between devices, shards(): lax.all_to_all(outgoing, 'site', split_axis=0, concat_axis=0, tiled=True)  10.3 us
  transfers between devices with their start and end apart: 5, of which 3 were waited for; matrix products, arithmetic and copies ran while one was open for 14% of the time, Pallas kernels for 2%

profile of v6, /device:TPU:0, one launch (start us, length us, event | category | flops | bytes accessed | tf_op | source)
XLA Modules:
  0.0 295.3 jit_solution(15508013061600818466)
XLA Ops:
  0.0 0.8 eq.54
  0.8 0.3 fusion.22
  1.1 0.1 broadcast_compare_fusion
  1.2 0.2 reduce_window_sum.18
  1.3 0.2 select_reduce_fusion.2
  1.5 0.7 copy.24.index_ref
  2.2 6.5 %shard_map.74 = bf16[8,5,336,256]{3,2,1,0:T(8,128)(2,1)} custom-call(s32[8,5]{1,0:T(8,128)} %copy.24.index_ref, bf16[336,2560]{1,0:T(8,128)(2,1)} %bitcast.74), custom_call_target="tpu_custom_call" | custom-call | bytes 13762560 | tf_op jit(solution)/shard_map/pallas_call | solution.py:27
  8.7 5.3 %all-to-all-start = ((bf16[8,5,336,256]{3,2,1,0:T(8,128)(2,1)}), bf16[8,5,336,256]{3,2,1,0:T(8,128)(2,1)}, u32[]{:S(2)}, u32[]{:S(2)}) async-start(bf16[8,5,336,256]{3,2,1,0:T(8,128)(2,1)} %shard_map.74), calls=%async_computation | async-start | bytes 13762560 | tf_op jit(solution)/shard_map/all_to_all | solution.py:171
  14.0 2.7 collective-permute-start.1
  16.8 2.6 collective-permute-start
  19.4 147.3 %collective-permute-done = bf16[2560,336]{0,1:T(8,128)(2,1)S(1)} collective-permute-done((bf16[2560,336]{0,1:T(8,128)(2,1)S(1)}, bf16[2560,336]{0,1:T(8,128)(2,1)S(1)}, u32[]{:S(2)}, u32[]{:S(2)}) %collective-permute-start) | collective-permute-done | bytes 1720352 | tf_op jit(solution)/shard_map/ppermute | solution.py:109
  166.6 1.2 copy-done.2
  167.8 6.4 %shard_map.73 = bf16[8,5,336,256]{3,2,1,0:T(8,128)(2,1)} custom-call(s32[8,5]{1,0:T(8,128)} %copy.24.index_ref, bf16[336,2560]{1,0:T(8,128)(2,1)} %bitcast.75), custom_call_target="tpu_custom_call" | custom-call | bytes 13762560 | tf_op jit(solution)/shard_map/pallas_call | solution.py:27
  174.3 0.0 all-to-all-done
  174.3 4.9 %all-to-all-start.1 = ((bf16[8,5,336,256]{3,2,1,0:T(8,128)(2,1)}), bf16[8,5,336,256]{3,2,1,0:T(8,128)(2,1)}, u32[]{:S(2)}, u32[]{:S(2)}) async-start(bf16[8,5,336,256]{3,2,1,0:T(8,128)(2,1)} %shard_map.73), calls=%async_computation.1 | async-start | bytes 13762560 | tf_op jit(solution)/shard_map/all_to_all | solution.py:171
  179.2 0.1 reshape.162
  179.3 0.2 reduce_window_sum.17
  179.5 0.1 sub.44
  179.6 0.7 constant_dynamic-slice_fusion.4
  180.3 0.2 select_reduce_fusion.1
  180.5 0.2 select_reduce_fusion
  180.7 0.1 compare_select_fusion
  180.7 0.1 reshape.165
  180.9 0.7 dynamic_slice.31
  181.6 0.1 constant_dynamic-slice_fusion
  181.6 0.1 eq.47
  181.7 0.1 eq.124
  181.8 10.3 %gather_fusion = bf16[160,64,256]{2,1,0:T(8,128)(2,1)} fusion(bf16[160,64,256]{2,1,0:T(8,128)(2,1)} %bitcast.67, s32[1024]{0:T(1024)S(1)} %pad_clamp_fusion), kind=kCustom, calls=%fused_computation | custom fusion | bytes 10486400 | tf_op jit(solution)/shard_map/gather | solution.py:146
  192.1 0.1 multiply_multiply_fusion
  192.1 0.0 collective-permute-done.1
  192.2 10.2 %gather_fusion.1 = bf16[160,64,256]{2,1,0:T(8,128)(2,1)} fusion(bf16[160,64,256]{2,1,0:T(8,128)(2,1)} %bitcast.11, s32[1024]{0:T(1024)S(1)} %pad_clamp_fusion), kind=kCustom, calls=%fused_computation.1 | custom fusion | bytes 10486400 | tf_op jit(solution)/shard_map/gather | solution.py:146
  202.4 7.4 %fusion.19 = bf16[4,64,336]{2,1,0:T(8,128)(2,1)S(1)} fusion(bf16[4,40,64,256]{3,2,1,0:T(8,128)(2,1)} %bitcast.72, bf16[40,336,256,1]{2,1,0,3:T(8,128)(2,1)} %bitcast.6), kind=kOutput, calls=%fused_computation.31 | convolution fusion | flops 1761693696 | bytes 12296192 | tf_op jit(solution)/shard_map/ksij,swj->kiw/dot_general | solution.py:179
  209.8 0.1 reshape.153
  209.9 0.3 fusion.15
  210.2 0.3 copy.29
  210.5 0.2 reshape.154
  210.7 7.4 %fusion.18 = bf16[4,64,336]{2,1,0:T(8,128)(2,1)S(1)} fusion(bf16[4,40,64,256]{3,2,1,0:T(8,128)(2,1)} %bitcast.68, bf16[40,336,256,1]{2,1,0,3:T(8,128)(2,1)} %bitcast.6), kind=kOutput, calls=%fused_computation.30 | convolution fusion | flops 1761693696 | bytes 12296192 | tf_op jit(solution)/shard_map/ksij,swj->kiw/dot_general | solution.py:179
  218.1 0.1 reshape.150
  218.2 0.3 fusion.14
  218.5 0.3 copy.27
  218.8 0.2 reshape.151
  218.9 0.3 fusion.24
  219.3 0.0 slice-start
  219.3 0.3 fusion.12
  219.6 0.9 copy.30
  220.5 36.6 %all-to-all-done.1 = bf16[8,5,336,256]{3,2,1,0:T(8,128)(2,1)} async-done(((bf16[8,5,336,256]{3,2,1,0:T(8,128)(2,1)}), bf16[8,5,336,256]{3,2,1,0:T(8,128)(2,1)}, u32[]{:S(2)}, u32[]{:S(2)}) %all-to-all-start.1) | async-done | bytes 6881312 | tf_op jit(solution)/shard_map/all_to_all | solution.py:171
  257.1 7.5 %fusion.21 = bf16[4,64,336]{2,1,0:T(8,128)(2,1)S(1)} fusion(bf16[4,40,64,256]{3,2,1,0:T(8,128)(2,1)} %bitcast.73, bf16[40,336,256,1]{2,1,0,3:T(8,128)(2,1)} %bitcast.19), kind=kOutput, calls=%fused_computation.33 | convolution fusion | flops 1761693696 | bytes 12296192 | tf_op jit(solution)/shard_map/ksij,swj->kiw/dot_general | solution.py:179
  264.7 5.1 %fusion.20 = bf16[4,64,336]{2,1,0:T(8,128)(2,1)S(1)} fusion(bf16[4,40,64,256]{3,2,1,0:T(8,128)(2,1)S(1)} %bitcast.71, bf16[40,336,256,1]{2,1,0,3:T(8,128)(2,1)} %bitcast.19), kind=kOutput, calls=%fused_computation.32 | convolution fusion | flops 1761693696 | bytes 12296192 | tf_op jit(solution)/shard_map/ksij,swj->kiw/dot_general | solution.py:179
  269.8 0.1 reshape.159
  269.9 0.3 fusion.17
  270.2 0.3 copy.34
  270.5 0.2 reshape.160
  270.7 0.1 reshape.157
  270.8 0.3 fusion.16
  271.1 0.3 copy.32
  271.4 0.2 reshape.158
  271.5 0.3 fusion.23
  271.9 0.3 fusion.13
  272.2 0.9 copy.35
  273.1 13.0 %shard_map.75 = f32[2,64,336]{2,1,0:T(8,128)} custom-call(bf16[8,64,336]{2,1,0:T(8,128)(2,1)} %bitcast.76, bf16[8,64,336]{2,1,0:T(8,128)(2,1)} %bitcast.77), custom_call_target="tpu_custom_call" | custom-call | tf_op jit(solution)/shard_map/pallas_call | solution.py:82
  286.2 0.9 slice_bitcast_fusion
  287.1 3.4 %collective-permute-start.2 = (f32[64,336]{1,0:T(8,128)S(1)}, f32[64,336]{1,0:T(8,128)S(1)}, u32[]{:S(2)}, u32[]{:S(2)}) collective-permute-start(f32[64,336]{1,0:T(8,128)S(1)} %slice_bitcast_fusion), channel_id=1, source_target_pairs={{0,2},{1,3},{2,0},{3,1},{4,6},{5,7},{6,4},{7,5},{8,10},{9,11},{10,... | collective-permute-start | bytes 258056 | tf_op jit(solution)/shard_map/ppermute | solution.py:200
  290.5 3.3 %collective-permute-done.2 = f32[64,336]{1,0:T(8,128)S(1)} collective-permute-done((f32[64,336]{1,0:T(8,128)S(1)}, f32[64,336]{1,0:T(8,128)S(1)}, u32[]{:S(2)}, u32[]{:S(2)}) %collective-permute-start.2) | collective-permute-done | bytes 86048 | tf_op jit(solution)/shard_map/ppermute | solution.py:200
  293.8 1.5 bitcast_add_fusion
  (22 shorter events, 0.1 us)
Async XLA Ops:
  0.0 209.9 %copy-start = (bf16[168,168]{1,0:T(8,128)(2,1)S(1)}, bf16[168,168]{1,0:T(8,128)(2,1)}, u32[]{:S(2)}) copy-start(bf16[168,168]{1,0:T(8,128)(2,1)} %param.10) | copy-start | bytes 169348
  8.7 8.1 %copy-start.1 = (bf16[2560,336]{0,1:T(8,128)(2,1)S(1)}, bf16[2560,336]{0,1:T(8,128)(2,1)}, u32[]{:S(2)}) copy-start(bf16[2560,336]{0,1:T(8,128)(2,1)} %param.7) | copy-start | bytes 5160964
  8.7 165.5 %all-to-all-start = ((bf16[8,5,336,256]{3,2,1,0:T(8,128)(2,1)}), bf16[8,5,336,256]{3,2,1,0:T(8,128)(2,1)}, u32[]{:S(2)}, u32[]{:S(2)}) async-start(bf16[8,5,336,256]{3,2,1,0:T(8,128)(2,1)} %shard_map.74), calls=%async_computation | async-start | bytes 13762560 | tf_op jit(solution)/shard_map/all_to_all | solution.py:171
  14.0 178.1 %collective-permute-start.1 = (bf16[4,40,64,256]{3,2,1,0:T(8,128)(2,1)}, bf16[4,40,64,256]{3,2,1,0:T(8,128)(2,1)}, u32[]{:S(2)}, u32[]{:S(2)}) collective-permute-start(bf16[4,40,64,256]{3,2,1,0:T(8,128)(2,1)} %param.9), channel_id=1, source_target_pairs={{0,1},{1,0},{2,3},{3,2},{4,5},{5,4},{6,7},{7,6},{8,9},{9,8},{10,11... | collective-permute-start | bytes 15728648 | tf_op jit(solution)/shard_map/ppermute | solution.py:115
  16.8 149.9 %collective-permute-start = (bf16[2560,336]{0,1:T(8,128)(2,1)S(1)}, bf16[2560,336]{0,1:T(8,128)(2,1)S(1)}, u32[]{:S(2)}, u32[]{:S(2)}) collective-permute-start(bf16[2560,336]{0,1:T(8,128)(2,1)S(1)} %copy-done.1), channel_id=1, source_target_pairs={{0,2},{1,3},{2,0},{3,1},{4,6},{5,7},{6,4},{7,5},{8,10},{9,11},{10,... | collective-permute-start | bytes 5160968 | tf_op jit(solution)/shard_map/ppermute | solution.py:109
  166.6 1.2 copy-start.2
  174.3 6.6 %copy-start.3 = (f32[1024]{0:T(1024)S(1)}, f32[1024]{0:T(1024)}, u32[]{:S(2)}) copy-start(f32[1024]{0:T(1024)} %param.11) | copy-start | bytes 12292
  174.3 6.6 %copy-start.4 = (f32[1024]{0:T(1024)S(1)}, f32[1024]{0:T(1024)}, u32[]{:S(2)}) copy-start(f32[1024]{0:T(1024)} %param.12) | copy-start | bytes 12292
  174.3 82.8 %all-to-all-start.1 = ((bf16[8,5,336,256]{3,2,1,0:T(8,128)(2,1)}), bf16[8,5,336,256]{3,2,1,0:T(8,128)(2,1)}, u32[]{:S(2)}, u32[]{:S(2)}) async-start(bf16[8,5,336,256]{3,2,1,0:T(8,128)(2,1)} %shard_map.73), calls=%async_computation.1 | async-start | bytes 13762560 | tf_op jit(solution)/shard_map/all_to_all | solution.py:171
  219.3 45.4 %slice-start = ((s8[5242880]{0:T(1024)(128)(4,1)}), s8[1048576]{0:T(1024)(128)(4,1)S(1)}, s32[]{:S(2)}) async-start(s8[5242880]{0:T(1024)(128)(4,1)} %bitcast.69), calls=%async_computation.2 | async-start | bytes 2097152
  257.1 7.6 %slice-start.1 = ((s8[5242880]{0:T(1024)(128)(4,1)}), s8[4194304]{0:T(1024)(128)(4,1)S(1)}, s32[]{:S(2)}) async-start(s8[5242880]{0:T(1024)(128)(4,1)} %bitcast.69), calls=%async_computation.3 | async-start | bytes 8388608
  287.1 6.7 %collective-permute-start.2 = (f32[64,336]{1,0:T(8,128)S(1)}, f32[64,336]{1,0:T(8,128)S(1)}, u32[]{:S(2)}, u32[]{:S(2)}) collective-permute-start(f32[64,336]{1,0:T(8,128)S(1)} %slice_bitcast_fusion), channel_id=1, source_target_pairs={{0,2},{1,3},{2,0},{3,1},{4,6},{5,7},{6,4},{7,5},{8,10},{9,11},{10,... | collective-permute-start | bytes 258056 | tf_op jit(solution)/shard_map/ppermute | solution.py:200
